TPU v7x, 32 devices: a whole 2x2x4 slice. The times are simulated.
32 devices in a mesh: ctx: 16 (over z, y, core), head: 2 (over x).
Axes of the slice: x: 2, y: 2, z: 4, core: 2. Of those that a mesh axis runs over, the one named last changes fastest.
Arguments:
- queries: bfloat16 [4096, 2048], P(('ctx', 'head')), may hold values from -200 to 200
- keys: bfloat16 [4096, 256], P(('ctx', 'head')), may hold values from -7 to 7
- values: bfloat16 [4096, 256], P(('ctx', 'head')), may hold values from -6 to 6
- output_cotangent: bfloat16 [4096, 2048], P(('ctx', 'head')), may hold values from -6 to 6
- doc_ids: int32 [4096], replicated, may hold values from 0 to 3, never falling along the last dimension, each value on 1 to 2048 neighbouring positions
Outputs:
- grad_queries: bfloat16 [4096, 2048], P(('ctx', 'head'))
- key_gradients: bfloat16 [4096, 256], P(('ctx', 'head'))
- value_gradients: bfloat16 [4096, 256], P(('ctx', 'head'))
Inputs may be any that keep to these rules, and one draw needn't show every extreme that they name: `doc_ids`: document numbers never fall along the tokens; every number occurs; each document has 1 to 2048 tokens and one has exactly 2048.
All inputs are finite; a program needn't handle non-finite values.
Results may differ from a plain program's by a relative error of at most 0.017.
Values may be sent and summed in bfloat16 or wider, within the bound.
A program may use at most 128 MiB of HBM per device.

v0:
```python
import jax
import jax.numpy as jnp
from jax import lax
from jax.sharding import PartitionSpec as P

SPAN = 8


masked_score = -1e30


def shifted(value, axis, steps):
    count = lax.axis_size(axis)
    leading, last = (max(0, -steps), min(count, count - steps))
    return lax.ppermute(value, axis, [(source, source + steps) for source in range(leading, last)])


def block_docs(doc_ids, block, length):
    block_count = doc_ids.shape[0] // length
    first_row = jnp.clip(block, 0, block_count - 1) * length
    return lax.dynamic_slice_in_dim(doc_ids, first_row, length, 0)


def tile_mask(query_docs, key_docs, offset, in_range):
    length = query_docs.shape[0]
    query_pos = lax.broadcasted_iota(jnp.int32, (length, length), 0)
    key_pos = lax.broadcasted_iota(jnp.int32, (length, length), 1)
    same_doc = query_docs[:, None] == key_docs[None, :]
    return same_doc & (key_pos <= query_pos + offset * length) & in_range


def scores_of(query_heads, key_block, scaling):
    return (
        jnp.einsum("qgd,kd->gqk", query_heads, key_block, preferred_element_type=jnp.float32)
        * scaling
    )


def tile_grads(scores, query_heads, grad_heads, key_block, value_block, allowed, log_norm, row_dot):
    weights = jnp.where(allowed[None], jnp.exp(scores - log_norm[:, :, None]), 0.0)
    rounded = weights.astype(jnp.bfloat16)
    grad_weights = jnp.einsum(
        "qgd,kd->gqk", grad_heads, value_block, preferred_element_type=jnp.float32
    )
    grad_scores = (weights * (grad_weights - row_dot[:, :, None])).astype(jnp.bfloat16)
    part_query = jnp.einsum(
        "gqk,kd->qgd", grad_scores, key_block, preferred_element_type=jnp.float32
    )
    part_key = jnp.einsum(
        "gqk,qgd->kd", grad_scores, query_heads, preferred_element_type=jnp.float32
    )
    part_value = jnp.einsum("gqk,qgd->kd", rounded, grad_heads, preferred_element_type=jnp.float32)
    return (part_query, part_key, part_value)


def on_device(queries, keys, values, output_cotangent, doc_ids):
    query_rows, grad_rows, key_rows, value_rows = (
        lax.all_to_all(queries, "head", split_axis=1, concat_axis=0, tiled=True),
        lax.all_to_all(output_cotangent, "head", split_axis=1, concat_axis=0, tiled=True),
        lax.all_to_all(keys, "head", split_axis=1, concat_axis=0, tiled=True),
        lax.all_to_all(values, "head", split_axis=1, concat_axis=0, tiled=True),
    )
    length = key_rows.shape[0]
    head_width = key_rows.shape[1]
    group_size = query_rows.shape[1] // head_width
    scaling = head_width ** (-0.5)
    own_block = lax.axis_index("ctx")
    query_heads = query_rows.reshape(length, group_size, head_width)
    grad_heads = grad_rows.reshape(length, group_size, head_width)
    own_docs = block_docs(doc_ids, own_block, length)
    key_window = key_rows[None]
    value_window = value_rows[None]
    for level_index in range(SPAN.bit_length() - 1):
        stride = 2**level_index
        got_keys, got_values = shifted((key_window, value_window), "ctx", stride)
        key_window = jnp.concatenate([key_window, got_keys], axis=0)
        value_window = jnp.concatenate([value_window, got_values], axis=0)
    last_keys, last_values = shifted((key_rows, value_rows), "ctx", SPAN)
    key_window = jnp.concatenate([key_window, last_keys[None]], axis=0)
    value_window = jnp.concatenate([value_window, last_values[None]], axis=0)

    def near_tile(offset):
        source = own_block - offset
        key_docs = block_docs(doc_ids, source, length)
        in_range = source >= 0
        active = in_range & (key_docs[length - 1] >= own_docs[0])
        allowed = tile_mask(own_docs, key_docs, offset, in_range)
        return (active, allowed, key_window[offset], value_window[offset])

    def stats_step(offset, carried):
        active, allowed, key_block, value_block = near_tile(offset)

        def stats_compute(current):
            row_max, row_sum, score_store = current
            scores = scores_of(query_heads, key_block, scaling)
            score_store = lax.dynamic_update_index_in_dim(score_store, scores, offset, 0)
            masked = jnp.where(allowed[None], scores, masked_score)
            new_max = jnp.maximum(row_max, jnp.max(masked, axis=2))
            row_sum = row_sum * jnp.exp(row_max - new_max) + jnp.sum(
                jnp.exp(masked - new_max[:, :, None]), axis=2
            )
            return (new_max, row_sum, score_store)

        return lax.cond(active, stats_compute, lambda current: current, carried)

    start_max = jnp.full((group_size, length), masked_score, jnp.float32)
    start_sum = jnp.zeros((group_size, length), jnp.float32)
    start_store = jnp.zeros((SPAN + 1, group_size, length, length), jnp.float32)
    row_max, row_sum, score_store = lax.fori_loop(
        0, SPAN + 1, stats_step, (start_max, start_sum, start_store)
    )
    log_norm = row_max + jnp.log(row_sum)

    def output_step(offset, carried):
        active, allowed, key_block, value_block = near_tile(offset)

        def output_compute(running):
            scores = lax.dynamic_index_in_dim(score_store, offset, 0, keepdims=False)
            weights = jnp.where(allowed[None], jnp.exp(scores - log_norm[:, :, None]), 0.0)
            return running + jnp.einsum(
                "gqk,kd->qgd",
                weights.astype(jnp.bfloat16),
                value_block,
                preferred_element_type=jnp.float32,
            )

        return lax.cond(active, output_compute, lambda running: running, carried)

    attn_out = lax.fori_loop(
        0, SPAN + 1, output_step, jnp.zeros((length, group_size, head_width), jnp.float32)
    )
    row_dot = jnp.transpose(jnp.sum(grad_heads.astype(jnp.float32) * attn_out, axis=2))
    near_reach = SPAN

    def grad_step(offset, carried):
        active, allowed, key_block, value_block = near_tile(offset)

        def grad_compute(current):
            grad_query, part_keys, part_values = current
            scores = lax.dynamic_index_in_dim(score_store, offset, 0, keepdims=False)
            part_query, part_key, part_value = tile_grads(
                scores, query_heads, grad_heads, key_block, value_block, allowed, log_norm, row_dot
            )
            part_keys = lax.dynamic_update_index_in_dim(part_keys, part_key, offset, 0)
            part_values = lax.dynamic_update_index_in_dim(part_values, part_value, offset, 0)
            return (grad_query + part_query, part_keys, part_values)

        return lax.cond(active, grad_compute, lambda current: current, carried)

    zero_query = jnp.zeros((length, group_size, head_width), jnp.float32)
    zero_parts = jnp.zeros((near_reach + 1, length, head_width), jnp.float32)
    grad_query, part_keys, part_values = lax.fori_loop(
        0, near_reach + 1, grad_step, (zero_query, zero_parts, zero_parts)
    )
    extra_zero = jnp.zeros((length, head_width), jnp.float32)
    extra_keys = extra_zero
    extra_values = extra_zero
    stack_len = max(near_reach, 1)
    stacked_keys = part_keys[:stack_len]
    stacked_values = part_values[:stack_len]
    back_keys, back_values = (
        shifted(part_keys[near_reach].astype(jnp.bfloat16), "ctx", -near_reach).astype(jnp.float32),
        shifted(part_values[near_reach].astype(jnp.bfloat16), "ctx", -near_reach).astype(
            jnp.float32
        ),
    )
    extra_keys = extra_keys + back_keys
    extra_values = extra_values + back_values
    for level_index in range(stack_len.bit_length() - 1):
        stride = stack_len // 2 ** (level_index + 1)
        back_keys, back_values = shifted(
            (stacked_keys[stride : 2 * stride], stacked_values[stride : 2 * stride]), "ctx", -stride
        )
        stacked_keys = stacked_keys[:stride] + back_keys
        stacked_values = stacked_values[:stride] + back_values
    key_total = stacked_keys[0]
    value_total = stacked_values[0]
    key_total = key_total + extra_keys
    value_total = value_total + extra_values
    grad_query_out = (
        (grad_query * scaling).astype(jnp.bfloat16).reshape(length, group_size * head_width)
    )
    grad_key_out = (key_total * scaling).astype(jnp.bfloat16)
    grad_value_out = value_total.astype(jnp.bfloat16)
    out_queries, out_keys, out_values = (
        lax.all_to_all(grad_query_out, "head", split_axis=0, concat_axis=1, tiled=True),
        lax.all_to_all(grad_key_out, "head", split_axis=0, concat_axis=1, tiled=True),
        lax.all_to_all(grad_value_out, "head", split_axis=0, concat_axis=1, tiled=True),
    )
    return (out_queries, out_keys, out_values)


def solution(mesh):
    in_specs = (
        P(("ctx", "head"), None),
        P(("ctx", "head"), None),
        P(("ctx", "head"), None),
        P(("ctx", "head"), None),
        P(),
    )
    out_specs = (P(("ctx", "head"), None), P(("ctx", "head"), None), P(("ctx", "head"), None))
    return jax.shard_map(
        on_device, mesh=mesh, in_specs=in_specs, out_specs=out_specs, check_vma=False
    )
```

profile of v0, /device:TPU:16, one launch (start us, length us, event | category | flops | bytes accessed | tf_op | source)
XLA Modules:
  0.0 339.3 jit_solution(7841062772822629406)
XLA Ops:
  11.4 3.3 all-to-all-start.2
  18.8 3.5 %all-to-all-start.1 = ((bf16[128,2,1024]{2,0,1:T(8,128)(2,1)}), bf16[128,2,1024]{2,0,1:T(8,128)(2,1)S(1)}, u32[]{:S(2)}, u32[]{:S(2)}) async-start(bf16[128,2,1024]{2,0,1:T(8,128)(2,1)} %bitcast.142), calls=%async_computation.1 | async-start | bytes 1048576 | tf_op jit(solution)/shard_map/all_to_all | solution.py:58
  26.4 3.4 %collective-permute-start.1 = (bf16[2,256,128]{2,1,0:T(8,128)(2,1)S(1)}, bf16[2,256,128]{2,1,0:T(8,128)(2,1)S(1)}, u32[]{:S(2)}, u32[]{:S(2)}) collective-permute-start(bf16[2,256,128]{2,1,0:T(8,128)(2,1)S(1)} %pad_maximum_fusion.2), channel_id=1, source_target_pairs={{0,4},{2,6},{4,8},{6,10},{8,12},{10,14},{12,16},{14,18},{16,20},{1... | collective-permute-start | bytes 393224 | tf_op jit(solution)/shard_map/ppermute | solution.py:15
  29.8 3.4 %collective-permute-start.5 = (bf16[2,256,128]{2,1,0:T(8,128)(2,1)S(1)}, bf16[2,256,128]{2,1,0:T(8,128)(2,1)S(1)}, u32[]{:S(2)}, u32[]{:S(2)}) collective-permute-start(bf16[2,256,128]{2,1,0:T(8,128)(2,1)S(1)} %pad_maximum_fusion.3), channel_id=1, source_target_pairs={{0,4},{2,6},{4,8},{6,10},{8,12},{10,14},{12,16},{14,18},{16,20},{1... | collective-permute-start | bytes 393224 | tf_op jit(solution)/shard_map/ppermute | solution.py:15
  33.3 3.3 collective-permute-done.1
  39.1 3.5 %all-to-all-start.3 = ((bf16[128,2,1024]{2,0,1:T(8,128)(2,1)}), bf16[128,2,1024]{2,0,1:T(8,128)(2,1)S(1)}, u32[]{:S(2)}, u32[]{:S(2)}) async-start(bf16[128,2,1024]{2,0,1:T(8,128)(2,1)} %bitcast.141), calls=%async_computation.3 | async-start | bytes 1048576 | tf_op jit(solution)/shard_map/all_to_all | solution.py:59
  44.8 6.1 %all-to-all-done.3 = bf16[128,2,1024]{2,0,1:T(8,128)(2,1)S(1)} async-done(((bf16[128,2,1024]{2,0,1:T(8,128)(2,1)}), bf16[128,2,1024]{2,0,1:T(8,128)(2,1)S(1)}, u32[]{:S(2)}, u32[]{:S(2)}) %all-to-all-start.3) | async-done | bytes 524320 | tf_op jit(solution)/shard_map/all_to_all | solution.py:59
  53.7 8.8 %broadcast_in_dim.112 = f32[9,8,256,256]{2,3,1,0:T(8,128)} broadcast(f32[]{:T(128)} %constant.213.clone.1), dimensions={} | broadcast | bytes 18874372 | tf_op jit(solution)/shard_map/broadcast_in_dim | solution.py:108
  62.5 49.9 %while.50 = (s32[]{:T(128)}, f32[8,256]{1,0:T(8,128)S(1)}, f32[8,256]{1,0:T(8,128)S(1)}, f32[9,8,256,256]{2,3,1,0:T(8,128)}, s32[]{:T(128)}, /*index=5*/s32[4096...) while((s32[]{:T(128)}, f32[8,256]{1,0:T(8,128)S(1)}, ...), condition=%wide.region_5.6_spmd, body=%wide.region_0.5_spmd.sunk | while | flops 138678544 | bytes 9814480 | solution.py:109
  112.4 18.9 %copy.62 = f32[9,8,256,256]{3,2,1,0:T(8,128)} copy(f32[9,8,256,256]{2,3,1,0:T(8,128)} %get-tuple-element.1486) | data formatting | bytes 37748736 | tf_op jit(solution)/shard_map/while | solution.py:129
  132.5 49.3 %while.51 = (s32[]{:T(128)}, f32[256,8,128]{2,0,1:T(8,128)S(1)}, s32[]{:T(128)}, s32[4096]{0:T(1024)}, s32[256]{0:T(256)S(1)}, /*index=5*/f32[9,8,256,256]{3,2,1...) while((s32[]{:T(128)}, f32[256,8,128]{2,0,1:T(8,128)S(1)}, ...), condition=%wide.region_9.10_spmd, body=%wide.region_6.9_spmd.sunk | while | flops 136315152 | bytes 4933000 | solution.py:129
  184.0 86.9 %while.52 = (s32[]{:T(128)}, f32[256,8,128]{2,0,1:T(8,128)S(1)}, f32[9,256,128]{2,1,0:T(8,128)S(1)}, f32[9,256,128]{2,1,0:T(8,128)}, s32[]{:T(128)}, /*index=5*/...) while((s32[]{:T(128)}, f32[256,8,128]{2,0,1:T(8,128)S(1)}, ...), condition=%wide.region_14.15_spmd, body=%wide.region_11.14_spmd.sunk | while | flops 541589760 | bytes 14256700 | solution.py:152
  187.3 7.2 %conditional.8 = ((f32[256,8,128]{2,0,1:T(8,128)S(1)}, f32[9,256,128]{2,1,0:T(8,128)S(1)}, f32[9,256,128]{2,1,0:T(8,128)})) conditional(s32[]{:T(128)} %convert_element_type.94, (f32[256,8,128]{2,0,1:T(8,128)S(1)}, f32[9,256,128]{2,1,0:T(8,128)S(1)}, f32[9,256,128]{2,1,0:T(8,128)}) %tuple.150, (s32[256]{0:T(256)S(1)}, s32[256]{0:T(256)S(1)}, ...), branch_computations={%region_12.12_spmd, %region_13.13_spmd} | conditional | flops 541589760 | bytes 13991031 | solution.py:148
  197.7 7.2 %conditional.8 = ((f32[256,8,128]{2,0,1:T(8,128)S(1)}, f32[9,256,128]{2,1,0:T(8,128)S(1)}, f32[9,256,128]{2,1,0:T(8,128)})) conditional(s32[]{:T(128)} %convert_element_type.94, (f32[256,8,128]{2,0,1:T(8,128)S(1)}, f32[9,256,128]{2,1,0:T(8,128)S(1)}, f32[9,256,128]{2,1,0:T(8,128)}) %tuple.150, (s32[256]{0:T(256)S(1)}, s32[256]{0:T(256)S(1)}, ...), branch_computations={%region_12.12_spmd, %region_13.13_spmd} | conditional | flops 541589760 | bytes 13991031 | solution.py:148
  208.1 7.2 %conditional.8 = ((f32[256,8,128]{2,0,1:T(8,128)S(1)}, f32[9,256,128]{2,1,0:T(8,128)S(1)}, f32[9,256,128]{2,1,0:T(8,128)})) conditional(s32[]{:T(128)} %convert_element_type.94, (f32[256,8,128]{2,0,1:T(8,128)S(1)}, f32[9,256,128]{2,1,0:T(8,128)S(1)}, f32[9,256,128]{2,1,0:T(8,128)}) %tuple.150, (s32[256]{0:T(256)S(1)}, s32[256]{0:T(256)S(1)}, ...), branch_computations={%region_12.12_spmd, %region_13.13_spmd} | conditional | flops 541589760 | bytes 13991031 | solution.py:148
  218.6 7.2 %conditional.8 = ((f32[256,8,128]{2,0,1:T(8,128)S(1)}, f32[9,256,128]{2,1,0:T(8,128)S(1)}, f32[9,256,128]{2,1,0:T(8,128)})) conditional(s32[]{:T(128)} %convert_element_type.94, (f32[256,8,128]{2,0,1:T(8,128)S(1)}, f32[9,256,128]{2,1,0:T(8,128)S(1)}, f32[9,256,128]{2,1,0:T(8,128)}) %tuple.150, (s32[256]{0:T(256)S(1)}, s32[256]{0:T(256)S(1)}, ...), branch_computations={%region_12.12_spmd, %region_13.13_spmd} | conditional | flops 541589760 | bytes 13991031 | solution.py:148
  229.0 7.2 %conditional.8 = ((f32[256,8,128]{2,0,1:T(8,128)S(1)}, f32[9,256,128]{2,1,0:T(8,128)S(1)}, f32[9,256,128]{2,1,0:T(8,128)})) conditional(s32[]{:T(128)} %convert_element_type.94, (f32[256,8,128]{2,0,1:T(8,128)S(1)}, f32[9,256,128]{2,1,0:T(8,128)S(1)}, f32[9,256,128]{2,1,0:T(8,128)}) %tuple.150, (s32[256]{0:T(256)S(1)}, s32[256]{0:T(256)S(1)}, ...), branch_computations={%region_12.12_spmd, %region_13.13_spmd} | conditional | flops 541589760 | bytes 13991031 | solution.py:148
  239.5 7.2 %conditional.8 = ((f32[256,8,128]{2,0,1:T(8,128)S(1)}, f32[9,256,128]{2,1,0:T(8,128)S(1)}, f32[9,256,128]{2,1,0:T(8,128)})) conditional(s32[]{:T(128)} %convert_element_type.94, (f32[256,8,128]{2,0,1:T(8,128)S(1)}, f32[9,256,128]{2,1,0:T(8,128)S(1)}, f32[9,256,128]{2,1,0:T(8,128)}) %tuple.150, (s32[256]{0:T(256)S(1)}, s32[256]{0:T(256)S(1)}, ...), branch_computations={%region_12.12_spmd, %region_13.13_spmd} | conditional | flops 541589760 | bytes 13991031 | solution.py:148
  249.9 7.2 %conditional.8 = ((f32[256,8,128]{2,0,1:T(8,128)S(1)}, f32[9,256,128]{2,1,0:T(8,128)S(1)}, f32[9,256,128]{2,1,0:T(8,128)})) conditional(s32[]{:T(128)} %convert_element_type.94, (f32[256,8,128]{2,0,1:T(8,128)S(1)}, f32[9,256,128]{2,1,0:T(8,128)S(1)}, f32[9,256,128]{2,1,0:T(8,128)}) %tuple.150, (s32[256]{0:T(256)S(1)}, s32[256]{0:T(256)S(1)}, ...), branch_computations={%region_12.12_spmd, %region_13.13_spmd} | conditional | flops 541589760 | bytes 13991031 | solution.py:148
  260.4 7.2 %conditional.8 = ((f32[256,8,128]{2,0,1:T(8,128)S(1)}, f32[9,256,128]{2,1,0:T(8,128)S(1)}, f32[9,256,128]{2,1,0:T(8,128)})) conditional(s32[]{:T(128)} %convert_element_type.94, (f32[256,8,128]{2,0,1:T(8,128)S(1)}, f32[9,256,128]{2,1,0:T(8,128)S(1)}, f32[9,256,128]{2,1,0:T(8,128)}) %tuple.150, (s32[256]{0:T(256)S(1)}, s32[256]{0:T(256)S(1)}, ...), branch_computations={%region_12.12_spmd, %region_13.13_spmd} | conditional | flops 541589760 | bytes 13991031 | solution.py:148
  293.8 3.5 %all-to-all-start.4 = ((bf16[2,128,1024]{2,1,0:T(8,128)(2,1)}), bf16[2,128,1024]{2,1,0:T(8,128)(2,1)S(1)}, u32[]{:S(2)}, u32[]{:S(2)}) async-start(bf16[2,128,1024]{2,1,0:T(8,128)(2,1)} %all_to_all.108), calls=%async_computation.4 | async-start | bytes 1048576 | tf_op jit(solution)/shard_map/all_to_all | solution.py:186
  298.3 21.4 %collective-permute-start.14 = (f32[1,256,128]{2,1,0:T(8,128)S(1)}, f32[1,256,128]{2,1,0:T(8,128)S(1)}, u32[]{:S(2)}, u32[]{:S(2)}) collective-permute-start(f32[1,256,128]{2,1,0:T(8,128)S(1)} %slice.114), channel_id=1, source_target_pairs={{2,0},{4,2},{6,4},{8,6},{10,8},{12,10},{14,12},{16,14},{18,16},{20... | collective-permute-start | bytes 393224 | tf_op jit(solution)/shard_map/ppermute | solution.py:15
  323.6 3.3 all-to-all-start.6
  327.6 3.4 %all-to-all-done.6 = bf16[2,128,128]{2,1,0:T(8,128)(2,1)S(1)} async-done(((bf16[2,128,128]{2,1,0:T(8,128)(2,1)}), bf16[2,128,128]{2,1,0:T(8,128)(2,1)S(1)}, u32[]{:S(2)}, u32[]{:S(2)}) %all-to-all-start.6) | async-done | bytes 65568 | tf_op jit(solution)/shard_map/all_to_all | solution.py:188
  (406 shorter events, 256.8 us)
Async XLA Ops:
  2.1 9.3 %all-to-all-start = ((bf16[128,2,128]{2,0,1:T(8,128)(2,1)}), bf16[128,2,128]{2,0,1:T(8,128)(2,1)S(1)}, u32[]{:S(2)}, u32[]{:S(2)}) async-start(bf16[128,2,128]{2,0,1:T(8,128)(2,1)} %copy_bitcast_fusion.3), calls=%async_computation | async-start | bytes 131072 | tf_op jit(solution)/shard_map/all_to_all | solution.py:60
  11.4 7.4 %all-to-all-start.2 = ((bf16[128,2,128]{2,0,1:T(8,128)(2,1)}), bf16[128,2,128]{2,0,1:T(8,128)(2,1)S(1)}, u32[]{:S(2)}, u32[]{:S(2)}) async-start(bf16[128,2,128]{2,0,1:T(8,128)(2,1)} %copy_bitcast_fusion.2), calls=%async_computation.2 | async-start | bytes 131072 | tf_op jit(solution)/shard_map/all_to_all | solution.py:61
  14.7 11.6 %collective-permute-start = (bf16[1,256,128]{2,1,0:T(8,128)(2,1)S(1)}, bf16[1,256,128]{2,1,0:T(8,128)(2,1)S(1)}, u32[]{:S(2)}, u32[]{:S(2)}) collective-permute-start(bf16[1,256,128]{2,1,0:T(8,128)(2,1)S(1)} %bitcast.161), channel_id=1, source_target_pairs={{0,2},{2,4},{4,6},{6,8},{8,10},{10,12},{12,14},{14,16},{16,18},{18... | collective-permute-start | bytes 196616 | tf_op jit(solution)/shard_map/ppermute | solution.py:15
  16.6 36.2 %collective-permute-start.3 = (bf16[256,128]{1,0:T(8,128)(2,1)S(1)}, bf16[256,128]{1,0:T(8,128)(2,1)}, u32[]{:S(2)}, u32[]{:S(2)}) collective-permute-start(bf16[256,128]{1,0:T(8,128)(2,1)S(1)} %bitcast.163), channel_id=1, source_target_pairs={{0,16},{2,18},{4,20},{6,22},{8,24},{10,26},{12,28},{14,30},{1,17},... | collective-permute-start | bytes 196616 | tf_op jit(solution)/shard_map/ppermute | solution.py:15
  18.8 20.3 %all-to-all-start.1 = ((bf16[128,2,1024]{2,0,1:T(8,128)(2,1)}), bf16[128,2,1024]{2,0,1:T(8,128)(2,1)S(1)}, u32[]{:S(2)}, u32[]{:S(2)}) async-start(bf16[128,2,1024]{2,0,1:T(8,128)(2,1)} %bitcast.142), calls=%async_computation.1 | async-start | bytes 1048576 | tf_op jit(solution)/shard_map/all_to_all | solution.py:58
  22.3 7.5 %collective-permute-start.4 = (bf16[1,256,128]{2,1,0:T(8,128)(2,1)S(1)}, bf16[1,256,128]{2,1,0:T(8,128)(2,1)S(1)}, u32[]{:S(2)}, u32[]{:S(2)}) collective-permute-start(bf16[1,256,128]{2,1,0:T(8,128)(2,1)S(1)} %bitcast.156), channel_id=1, source_target_pairs={{0,2},{2,4},{4,6},{6,8},{8,10},{10,12},{12,14},{14,16},{16,18},{18... | collective-permute-start | bytes 196616 | tf_op jit(solution)/shard_map/ppermute | solution.py:15
  25.0 107.3 %collective-permute-start.7 = (bf16[256,128]{1,0:T(8,128)(2,1)S(1)}, bf16[256,128]{1,0:T(8,128)(2,1)S(1)}, u32[]{:S(2)}, u32[]{:S(2)}) collective-permute-start(bf16[256,128]{1,0:T(8,128)(2,1)S(1)} %bitcast.157), channel_id=1, source_target_pairs={{0,16},{2,18},{4,20},{6,22},{8,24},{10,26},{12,28},{14,30},{1,17},... | collective-permute-start | bytes 196616 | tf_op jit(solution)/shard_map/ppermute | solution.py:15
  26.4 10.3 %collective-permute-start.1 = (bf16[2,256,128]{2,1,0:T(8,128)(2,1)S(1)}, bf16[2,256,128]{2,1,0:T(8,128)(2,1)S(1)}, u32[]{:S(2)}, u32[]{:S(2)}) collective-permute-start(bf16[2,256,128]{2,1,0:T(8,128)(2,1)S(1)} %pad_maximum_fusion.2), channel_id=1, source_target_pairs={{0,4},{2,6},{4,8},{6,10},{8,12},{10,14},{12,16},{14,18},{16,20},{1... | collective-permute-start | bytes 393224 | tf_op jit(solution)/shard_map/ppermute | solution.py:15
  29.8 12.8 %collective-permute-start.5 = (bf16[2,256,128]{2,1,0:T(8,128)(2,1)S(1)}, bf16[2,256,128]{2,1,0:T(8,128)(2,1)S(1)}, u32[]{:S(2)}, u32[]{:S(2)}) collective-permute-start(bf16[2,256,128]{2,1,0:T(8,128)(2,1)S(1)} %pad_maximum_fusion.3), channel_id=1, source_target_pairs={{0,4},{2,6},{4,8},{6,10},{8,12},{10,14},{12,16},{14,18},{16,20},{1... | collective-permute-start | bytes 393224 | tf_op jit(solution)/shard_map/ppermute | solution.py:15
  36.6 15.2 %collective-permute-start.2 = (bf16[4,256,128]{2,1,0:T(8,128)(2,1)S(1)}, bf16[4,256,128]{2,1,0:T(8,128)(2,1)}, u32[]{:S(2)}, u32[]{:S(2)}) collective-permute-start(bf16[4,256,128]{2,1,0:T(8,128)(2,1)S(1)} %pad_maximum_fusion), channel_id=1, source_target_pairs={{0,8},{2,10},{4,12},{6,14},{8,16},{10,18},{12,20},{14,22},{16,24},... | collective-permute-start | bytes 786440 | tf_op jit(solution)/shard_map/ppermute | solution.py:15
  39.1 11.8 %all-to-all-start.3 = ((bf16[128,2,1024]{2,0,1:T(8,128)(2,1)}), bf16[128,2,1024]{2,0,1:T(8,128)(2,1)S(1)}, u32[]{:S(2)}, u32[]{:S(2)}) async-start(bf16[128,2,1024]{2,0,1:T(8,128)(2,1)} %bitcast.141), calls=%async_computation.3 | async-start | bytes 1048576 | tf_op jit(solution)/shard_map/all_to_all | solution.py:59
  42.6 88.7 %collective-permute-start.6 = (bf16[4,256,128]{2,1,0:T(8,128)(2,1)S(1)}, bf16[4,256,128]{2,1,0:T(8,128)(2,1)}, u32[]{:S(2)}, u32[]{:S(2)}) collective-permute-start(bf16[4,256,128]{2,1,0:T(8,128)(2,1)S(1)} %pad_maximum_fusion.1), channel_id=1, source_target_pairs={{0,8},{2,10},{4,12},{6,14},{8,16},{10,18},{12,20},{14,22},{16,24},... | collective-permute-start | bytes 786440 | tf_op jit(solution)/shard_map/ppermute | solution.py:15
  271.9 11.1 %collective-permute-start.12 = (f32[4,256,128]{2,1,0:T(8,128)S(1)}, f32[4,256,128]{2,1,0:T(8,128)S(1)}, u32[]{:S(2)}, u32[]{:S(2)}) collective-permute-start(f32[4,256,128]{2,1,0:T(8,128)S(1)} %slice.100), channel_id=1, source_target_pairs={{8,0},{10,2},{12,4},{14,6},{16,8},{18,10},{20,12},{22,14},{24,16},... | collective-permute-start | bytes 1572872 | tf_op jit(solution)/shard_map/ppermute | solution.py:15
  273.9 15.5 %collective-permute-start.8 = (f32[4,256,128]{2,1,0:T(8,128)S(1)}, f32[4,256,128]{2,1,0:T(8,128)S(1)}, u32[]{:S(2)}, u32[]{:S(2)}) collective-permute-start(f32[4,256,128]{2,1,0:T(8,128)S(1)} %slice.93), channel_id=1, source_target_pairs={{8,0},{10,2},{12,4},{14,6},{16,8},{18,10},{20,12},{22,14},{24,16},... | collective-permute-start | bytes 1572872 | tf_op jit(solution)/shard_map/ppermute | solution.py:15
  276.8 44.9 %collective-permute-start.15 = (bf16[256,128]{1,0:T(8,128)(2,1)S(1)}, bf16[256,128]{1,0:T(8,128)(2,1)}, u32[]{:S(2)}, u32[]{:S(2)}) collective-permute-start(bf16[256,128]{1,0:T(8,128)(2,1)S(1)} %fusion.43), channel_id=1, source_target_pairs={{16,0},{18,2},{20,4},{22,6},{24,8},{26,10},{28,12},{30,14},{17,1},... | collective-permute-start | bytes 196616 | tf_op jit(solution)/shard_map/ppermute | solution.py:15
  278.7 48.3 %collective-permute-start.11 = (bf16[256,128]{1,0:T(8,128)(2,1)S(1)}, bf16[256,128]{1,0:T(8,128)(2,1)S(1)}, u32[]{:S(2)}, u32[]{:S(2)}) collective-permute-start(bf16[256,128]{1,0:T(8,128)(2,1)S(1)} %fusion.42), channel_id=1, source_target_pairs={{16,0},{18,2},{20,4},{22,6},{24,8},{26,10},{28,12},{30,14},{17,1},... | collective-permute-start | bytes 196616 | tf_op jit(solution)/shard_map/ppermute | solution.py:15
  284.9 12.4 %collective-permute-start.13 = (f32[2,256,128]{2,1,0:T(8,128)}, f32[2,256,128]{2,1,0:T(8,128)}, u32[]{:S(2)}, u32[]{:S(2)}) collective-permute-start(f32[2,256,128]{2,1,0:T(8,128)} %slice.112), channel_id=1, source_target_pairs={{4,0},{6,2},{8,4},{10,6},{12,8},{14,10},{16,12},{18,14},{20,16},{2... | collective-permute-start | bytes 786440 | tf_op jit(solution)/shard_map/ppermute | solution.py:15
  290.3 29.3 %collective-permute-start.9 = (f32[2,256,128]{2,1,0:T(8,128)S(1)}, f32[2,256,128]{2,1,0:T(8,128)S(1)}, u32[]{:S(2)}, u32[]{:S(2)}) collective-permute-start(f32[2,256,128]{2,1,0:T(8,128)S(1)} %slice.107), channel_id=1, source_target_pairs={{4,0},{6,2},{8,4},{10,6},{12,8},{14,10},{16,12},{18,14},{20,16},{2... | collective-permute-start | bytes 786440 | tf_op jit(solution)/shard_map/ppermute | solution.py:15
  292.4 27.3 %copy-start.2 = (f32[4,256,128]{2,1,0:T(8,128)S(1)}, f32[4,256,128]{2,1,0:T(8,128)}, u32[]{:S(2)}) copy-start(f32[4,256,128]{2,1,0:T(8,128)} %copy-done.1) | copy-start | bytes 1572868
  293.8 29.9 %all-to-all-start.4 = ((bf16[2,128,1024]{2,1,0:T(8,128)(2,1)}), bf16[2,128,1024]{2,1,0:T(8,128)(2,1)S(1)}, u32[]{:S(2)}, u32[]{:S(2)}) async-start(bf16[2,128,1024]{2,1,0:T(8,128)(2,1)} %all_to_all.108), calls=%async_computation.4 | async-start | bytes 1048576 | tf_op jit(solution)/shard_map/all_to_all | solution.py:186
  298.3 23.9 %collective-permute-start.14 = (f32[1,256,128]{2,1,0:T(8,128)S(1)}, f32[1,256,128]{2,1,0:T(8,128)S(1)}, u32[]{:S(2)}, u32[]{:S(2)}) collective-permute-start(f32[1,256,128]{2,1,0:T(8,128)S(1)} %slice.114), channel_id=1, source_target_pairs={{2,0},{4,2},{6,4},{8,6},{10,8},{12,10},{14,12},{16,14},{18,16},{20... | collective-permute-start | bytes 393224 | tf_op jit(solution)/shard_map/ppermute | solution.py:15
  319.7 7.2 %collective-permute-start.10 = (f32[1,256,128]{2,1,0:T(8,128)S(1)}, f32[1,256,128]{2,1,0:T(8,128)S(1)}, u32[]{:S(2)}, u32[]{:S(2)}) collective-permute-start(f32[1,256,128]{2,1,0:T(8,128)S(1)} %slice.109), channel_id=1, source_target_pairs={{2,0},{4,2},{6,4},{8,6},{10,8},{12,10},{14,12},{16,14},{18,16},{20... | collective-permute-start | bytes 393224 | tf_op jit(solution)/shard_map/ppermute | solution.py:15
  323.6 7.4 %all-to-all-start.6 = ((bf16[2,128,128]{2,1,0:T(8,128)(2,1)}), bf16[2,128,128]{2,1,0:T(8,128)(2,1)S(1)}, u32[]{:S(2)}, u32[]{:S(2)}) async-start(bf16[2,128,128]{2,1,0:T(8,128)(2,1)} %bitcast.44), calls=%async_computation.6 | async-start | bytes 131072 | tf_op jit(solution)/shard_map/all_to_all | solution.py:188
  331.0 7.4 %all-to-all-start.5 = ((bf16[2,128,128]{2,1,0:T(8,128)(2,1)}), bf16[2,128,128]{2,1,0:T(8,128)(2,1)S(1)}, u32[]{:S(2)}, u32[]{:S(2)}) async-start(bf16[2,128,128]{2,1,0:T(8,128)(2,1)} %bitcast.39), calls=%async_computation.5 | async-start | bytes 131072 | tf_op jit(solution)/shard_map/all_to_all | solution.py:187
  (12 other events, 37.0 us)
where the time goes:
time: 335 us; the launch traced here: 339 us
  local copies, waits for them, and re-layouts  101 us (30%)
  matrix products  78.4 us (23%)
  starting transfers between devices  76.2 us (23%)
  loops' own time  36.7 us (11%)
  other arithmetic  24.2 us (7%)
  waiting for transfers between devices  21.8 us (7%)
    ppermute x16, starting transfers between devices, shifted(): lax.ppermute(value, axis, [(source, source + steps) for source in range(l...  52.5 us
    slice x54, local copies, waits for them, and re-layouts, near_tile(): active = in_range & (key_docs[length - 1] >= own_docs[0])  30.7 us
    dot_general x8, matrix products, tile_grads(): jnp.einsum('gqk,qgd->kd', rounded, grad_heads, preferred_element_type=jnp...  21.6 us
    dynamic_slice x28, local copies, waits for them, and re-layouts, block_docs(): return lax.dynamic_slice_in_dim(doc_ids, first_row, length, 0)  21.3 us
    dot_general x8, matrix products, tile_grads(): jnp.einsum('qgd,kd->gqk', grad_heads, value_block, preferred_element_type...  19.3 us
    while x1, local copies, waits for them, and re-layouts, on_device(): lax.fori_loop(0, SPAN + 1, output_step, jnp.zeros((length, group_size, he...  18.9 us
    dot_general x8, matrix products, output_compute(): jnp.einsum('gqk,kd->qgd', weights.astype(jnp.bfloat16), value_block, pref...  18.5 us
    dynamic_update_slice x8, other arithmetic, stats_compute(): lax.dynamic_update_index_in_dim(score_store, scores, offset, 0)  12.3 us
  transfers between devices with their start and end apart: 23, of which 8 were waited for; matrix products, arithmetic and copies ran while one was open for 25% of the time, Pallas kernels for 0%

commit v1 on v0

v1 whole, which is shorter than its diff:
```python
import functools
import math

import jax
import jax.numpy as jnp
from jax import lax
from jax.experimental import pallas as pl
from jax.experimental.pallas import tpu as pltpu
from jax.sharding import PartitionSpec as P

SPAN = 8


masked_score = -1e30
LOG2E = math.log2(math.e)


def shifted(value, axis, steps):
    count = lax.axis_size(axis)
    leading, last = (max(0, -steps), min(count, count - steps))
    return lax.ppermute(value, axis, [(source, source + steps) for source in range(leading, last)])


def block_docs(doc_ids, block, length):
    block_count = doc_ids.shape[0] // length
    first_row = jnp.clip(block, 0, block_count - 1) * length
    return lax.dynamic_slice_in_dim(doc_ids, first_row, length, 0)


def attention_kernel(
    query_ref, grad_ref, key_ref, value_ref, bound_ref, dq_ref, dk_ref, dv_ref, bias_ref, key_t_ref, value_t_ref,
    *, scaling
):
    window, width = key_ref.shape
    length = query_ref.shape[0]
    group_size = query_ref.shape[1] // width
    own_block = lax.axis_index("ctx")
    key_row = lax.broadcasted_iota(jnp.int32, (window, length), 0)
    key_pos = (own_block - key_row // length) * length + key_row % length
    query_pos = own_block * length + lax.broadcasted_iota(jnp.int32, (1, length), 1)
    allowed = (key_pos >= bound_ref[...]) & (key_pos <= query_pos)
    bias_ref[...] = jnp.where(allowed, 0.0, masked_score)
    key_t_ref[...] = key_ref[...].T
    value_t_ref[...] = value_ref[...].T
    dk_ref[...] = jnp.zeros_like(dk_ref)
    dv_ref[...] = jnp.zeros_like(dv_ref)
    contract_last = (((1,), (1,)), ((), ()))

    @pl.loop(0, group_size)
    def _(g):
        cols = pl.ds(pl.multiple_of(g * width, width), width)
        query = query_ref[:, cols]
        grad = grad_ref[:, cols]
        scores = lax.dot_general(key_ref[...], query, contract_last, preferred_element_type=jnp.float32)
        scores = scores * (scaling * LOG2E) + bias_ref[...]
        powers = jnp.exp2(scores - jnp.max(scores, axis=0, keepdims=True))
        weights = powers * (1.0 / jnp.sum(powers, axis=0, keepdims=True))
        rounded = weights.astype(jnp.bfloat16)
        out_t = jnp.dot(value_t_ref[...], rounded, preferred_element_type=jnp.float32)
        row_dot = jnp.sum(grad.astype(jnp.float32).T * out_t, axis=0, keepdims=True)
        grad_weights = lax.dot_general(value_ref[...], grad, contract_last, preferred_element_type=jnp.float32)
        grad_scores = (weights * (grad_weights - row_dot)).astype(jnp.bfloat16)
        dq_t = jnp.dot(key_t_ref[...], grad_scores, preferred_element_type=jnp.float32)
        dq_ref[:, cols] = (dq_t * scaling).T.astype(jnp.bfloat16)
        dk_ref[...] += jnp.dot(grad_scores, query, preferred_element_type=jnp.float32)
        dv_ref[...] += jnp.dot(rounded, grad, preferred_element_type=jnp.float32)

    dk_ref[...] = dk_ref[...] * scaling


def attention(query_rows, grad_rows, key_window, value_window, bound):
    length = query_rows.shape[0]
    window, width = key_window.shape
    vmem = pl.BlockSpec(memory_space=pltpu.VMEM)
    return pl.pallas_call(
        functools.partial(attention_kernel, scaling=width ** (-0.5)),
        out_shape=(
            jax.ShapeDtypeStruct(query_rows.shape, jnp.bfloat16),
            jax.ShapeDtypeStruct((window, width), jnp.float32),
            jax.ShapeDtypeStruct((window, width), jnp.float32),
        ),
        in_specs=[vmem] * 5,
        out_specs=(vmem,) * 3,
        scratch_shapes=[
            pltpu.VMEM((window, length), jnp.float32),
            pltpu.VMEM((width, window), jnp.bfloat16),
            pltpu.VMEM((width, window), jnp.bfloat16),
        ],
        compiler_params=pltpu.CompilerParams(vmem_limit_bytes=56 * 1024 * 1024),
    )(query_rows, grad_rows, key_window, value_window, bound)


def on_device(queries, keys, values, output_cotangent, doc_ids):
    query_rows, grad_rows, key_rows, value_rows = (
        lax.all_to_all(queries, "head", split_axis=1, concat_axis=0, tiled=True),
        lax.all_to_all(output_cotangent, "head", split_axis=1, concat_axis=0, tiled=True),
        lax.all_to_all(keys, "head", split_axis=1, concat_axis=0, tiled=True),
        lax.all_to_all(values, "head", split_axis=1, concat_axis=0, tiled=True),
    )
    length = key_rows.shape[0]
    head_width = key_rows.shape[1]
    own_block = lax.axis_index("ctx")
    key_window = key_rows[None]
    value_window = value_rows[None]
    for level_index in range(SPAN.bit_length() - 1):
        stride = 2**level_index
        got_keys, got_values = shifted((key_window, value_window), "ctx", stride)
        key_window = jnp.concatenate([key_window, got_keys], axis=0)
        value_window = jnp.concatenate([value_window, got_values], axis=0)
    last_keys, last_values = shifted((key_rows, value_rows), "ctx", SPAN)
    key_window = jnp.concatenate([key_window, last_keys[None]], axis=0)
    value_window = jnp.concatenate([value_window, last_values[None]], axis=0)

    own_docs = block_docs(doc_ids, own_block, length)
    bound = jnp.sum((doc_ids[:, None] < own_docs[None, :]).astype(jnp.int32), axis=0)[None]
    near_reach = SPAN
    grad_query_out, part_keys, part_values = attention(
        query_rows,
        grad_rows,
        key_window.reshape(-1, head_width),
        value_window.reshape(-1, head_width),
        bound,
    )
    part_keys = part_keys.reshape(near_reach + 1, length, head_width)
    part_values = part_values.reshape(near_reach + 1, length, head_width)
    extra_zero = jnp.zeros((length, head_width), jnp.float32)
    extra_keys = extra_zero
    extra_values = extra_zero
    stack_len = max(near_reach, 1)
    stacked_keys = part_keys[:stack_len]
    stacked_values = part_values[:stack_len]
    back_keys, back_values = (
        shifted(part_keys[near_reach].astype(jnp.bfloat16), "ctx", -near_reach).astype(jnp.float32),
        shifted(part_values[near_reach].astype(jnp.bfloat16), "ctx", -near_reach).astype(
            jnp.float32
        ),
    )
    extra_keys = extra_keys + back_keys
    extra_values = extra_values + back_values
    for level_index in range(stack_len.bit_length() - 1):
        stride = stack_len // 2 ** (level_index + 1)
        back_keys, back_values = shifted(
            (stacked_keys[stride : 2 * stride], stacked_values[stride : 2 * stride]), "ctx", -stride
        )
        stacked_keys = stacked_keys[:stride] + back_keys
        stacked_values = stacked_values[:stride] + back_values
    key_total = stacked_keys[0]
    value_total = stacked_values[0]
    key_total = key_total + extra_keys
    value_total = value_total + extra_values
    grad_key_out = key_total.astype(jnp.bfloat16)
    grad_value_out = value_total.astype(jnp.bfloat16)
    out_queries, out_keys, out_values = (
        lax.all_to_all(grad_query_out, "head", split_axis=0, concat_axis=1, tiled=True),
        lax.all_to_all(grad_key_out, "head", split_axis=0, concat_axis=1, tiled=True),
        lax.all_to_all(grad_value_out, "head", split_axis=0, concat_axis=1, tiled=True),
    )
    return (out_queries, out_keys, out_values)


def solution(mesh):
    in_specs = (
        P(("ctx", "head"), None),
        P(("ctx", "head"), None),
        P(("ctx", "head"), None),
        P(("ctx", "head"), None),
        P(),
    )
    out_specs = (P(("ctx", "head"), None), P(("ctx", "head"), None), P(("ctx", "head"), None))
    return jax.shard_map(
        on_device, mesh=mesh, in_specs=in_specs, out_specs=out_specs, check_vma=False
    )
```

time: 335 us -> 157 us (0.47)
  the two profiles are of different devices: /device:TPU:16 before, /device:TPU:0 now
where the time goes in v1:
time: 157 us; the launch traced here: 155 us
  starting transfers between devices  61.6 us (39%)
  waiting for transfers between devices  43.8 us (28%)
  Pallas kernels  29.8 us (19%)
  local copies, waits for them, and re-layouts  14.3 us (9%)
  other arithmetic  4.57 us (3%)
    ppermute x16, starting transfers between devices, shifted(): lax.ppermute(value, axis, [(source, source + steps) for source in range(l...  37 us
    ppermute x16, waiting for transfers between devices, shifted(): lax.ppermute(value, axis, [(source, source + steps) for source in range(l...  31.1 us
    pallas_call x1, Pallas kernels, attention(): pl.pallas_call(functools.partial(attention_kernel, scaling=width ** (-0.5...  29.8 us
    all_to_all x1, waiting for transfers between devices, on_device(): lax.all_to_all(output_cotangent, 'head', split_axis=1, concat_axis=0, til...  5.82 us
    all_to_all x1, starting transfers between devices, on_device(): lax.all_to_all(values, 'head', split_axis=1, concat_axis=0, tiled=True)  4.23 us
    all_to_all x1, starting transfers between devices, on_device(): lax.all_to_all(queries, 'head', split_axis=1, concat_axis=0, tiled=True)  3.5 us
    all_to_all x1, starting transfers between devices, on_device(): lax.all_to_all(output_cotangent, 'head', split_axis=1, concat_axis=0, til...  3.5 us
    all_to_all x1, starting transfers between devices, on_device(): lax.all_to_all(grad_query_out, 'head', split_axis=0, concat_axis=1, tiled...  3.5 us
  transfers between devices with their start and end apart: 23, of which 10 were waited for; matrix products, arithmetic and copies ran while one was open for 9% of the time, Pallas kernels for 0%

profile of v1, /device:TPU:0, one launch (start us, length us, event | category | flops | bytes accessed | tf_op | source)
XLA Modules:
  0.0 155.2 jit_solution(1672462426065503444)
XLA Ops:
  2.4 4.2 %all-to-all-start.3 = ((bf16[128,2,128]{2,0,1:T(8,128)(2,1)}), bf16[128,2,128]{2,0,1:T(8,128)(2,1)S(1)}, u32[]{:S(2)}, u32[]{:S(2)}) async-start(bf16[128,2,128]{2,0,1:T(8,128)(2,1)} %copy.36), calls=%async_computation.3 | async-start | bytes 131072 | tf_op jit(solution)/shard_map/all_to_all | solution.py:98
  7.4 3.0 %convert_reduce_fusion = s32[256]{0:T(256)} fusion(s32[256]{0:T(256)S(1)} %dynamic_slice.3, s32[4096]{0:T(1024)} %param.9), kind=kLoop, calls=%fused_computation | loop fusion | flops 3145472 | bytes 18432 | tf_op jit(solution)/shard_map/reduce_sum | solution.py:115
  14.8 3.3 %all-to-all-start.2 = ((bf16[128,2,128]{2,0,1:T(8,128)(2,1)}), bf16[128,2,128]{2,0,1:T(8,128)(2,1)S(1)}, u32[]{:S(2)}, u32[]{:S(2)}) async-start(bf16[128,2,128]{2,0,1:T(8,128)(2,1)} %copy.34), calls=%async_computation.2 | async-start | bytes 131072 | tf_op jit(solution)/shard_map/all_to_all | solution.py:97
  19.6 5.5 %collective-permute-start.7 = (bf16[256,128]{1,0:T(8,128)(2,1)S(1)}, bf16[256,128]{1,0:T(8,128)(2,1)S(1)}, u32[]{:S(2)}, u32[]{:S(2)}) collective-permute-start(bf16[256,128]{1,0:T(8,128)(2,1)S(1)} %bitcast.74), channel_id=1, source_target_pairs={{0,16},{2,18},{4,20},{6,22},{8,24},{10,26},{12,28},{14,30},{1,17},... | collective-permute-start | bytes 196616 | tf_op jit(solution)/shard_map/ppermute | solution.py:21
  25.1 3.5 %all-to-all-start = ((bf16[128,2,1024]{2,0,1:T(8,128)(2,1)}), bf16[128,2,1024]{2,0,1:T(8,128)(2,1)S(1)}, u32[]{:S(2)}, u32[]{:S(2)}) async-start(bf16[128,2,1024]{2,0,1:T(8,128)(2,1)} %bitcast.66), calls=%async_computation | async-start | bytes 1048576 | tf_op jit(solution)/shard_map/all_to_all | solution.py:95
  28.6 2.1 %collective-permute-start.3 = (bf16[256,128]{1,0:T(8,128)(2,1)S(1)}, bf16[256,128]{1,0:T(8,128)(2,1)S(1)}, u32[]{:S(2)}, u32[]{:S(2)}) collective-permute-start(bf16[256,128]{1,0:T(8,128)(2,1)S(1)} %bitcast.77), channel_id=1, source_target_pairs={{0,16},{2,18},{4,20},{6,22},{8,24},{10,26},{12,28},{14,30},{1,17},... | collective-permute-start | bytes 196616 | tf_op jit(solution)/shard_map/ppermute | solution.py:21
  30.8 2.4 %collective-permute-start = (bf16[1,256,128]{2,1,0:T(8,128)(2,1)S(1)}, bf16[1,256,128]{2,1,0:T(8,128)(2,1)S(1)}, u32[]{:S(2)}, u32[]{:S(2)}) collective-permute-start(bf16[1,256,128]{2,1,0:T(8,128)(2,1)S(1)} %bitcast.78), channel_id=1, source_target_pairs={{0,2},{2,4},{4,6},{6,8},{8,10},{10,12},{12,14},{14,16},{16,18},{18... | collective-permute-start | bytes 196616 | tf_op jit(solution)/shard_map/ppermute | solution.py:21
  33.3 3.4 %collective-permute-start.5 = (bf16[2,256,128]{2,1,0:T(8,128)(2,1)S(1)}, bf16[2,256,128]{2,1,0:T(8,128)(2,1)S(1)}, u32[]{:S(2)}, u32[]{:S(2)}) collective-permute-start(bf16[2,256,128]{2,1,0:T(8,128)(2,1)S(1)} %pad_maximum_fusion.3), channel_id=1, source_target_pairs={{0,4},{2,6},{4,8},{6,10},{8,12},{10,14},{12,16},{14,18},{16,20},{1... | collective-permute-start | bytes 393224 | tf_op jit(solution)/shard_map/ppermute | solution.py:21
  36.7 3.4 %collective-permute-start.1 = (bf16[2,256,128]{2,1,0:T(8,128)(2,1)S(1)}, bf16[2,256,128]{2,1,0:T(8,128)(2,1)S(1)}, u32[]{:S(2)}, u32[]{:S(2)}) collective-permute-start(bf16[2,256,128]{2,1,0:T(8,128)(2,1)S(1)} %pad_maximum_fusion.2), channel_id=1, source_target_pairs={{0,4},{2,6},{4,8},{6,10},{8,12},{10,14},{12,16},{14,18},{16,20},{1... | collective-permute-start | bytes 393224 | tf_op jit(solution)/shard_map/ppermute | solution.py:21
  40.4 5.4 %collective-permute-start.6 = (bf16[4,256,128]{2,1,0:T(8,128)(2,1)S(1)}, bf16[4,256,128]{2,1,0:T(8,128)(2,1)S(1)}, u32[]{:S(2)}, u32[]{:S(2)}) collective-permute-start(bf16[4,256,128]{2,1,0:T(8,128)(2,1)S(1)} %pad_maximum_fusion.1), channel_id=1, source_target_pairs={{0,8},{2,10},{4,12},{6,14},{8,16},{10,18},{12,20},{14,22},{16,24},... | collective-permute-start | bytes 786440 | tf_op jit(solution)/shard_map/ppermute | solution.py:21
  45.8 2.9 %collective-permute-start.2 = (bf16[4,256,128]{2,1,0:T(8,128)(2,1)S(1)}, bf16[4,256,128]{2,1,0:T(8,128)(2,1)S(1)}, u32[]{:S(2)}, u32[]{:S(2)}) collective-permute-start(bf16[4,256,128]{2,1,0:T(8,128)(2,1)S(1)} %pad_maximum_fusion), channel_id=1, source_target_pairs={{0,8},{2,10},{4,12},{6,14},{8,16},{10,18},{12,20},{14,22},{16,24},... | collective-permute-start | bytes 786440 | tf_op jit(solution)/shard_map/ppermute | solution.py:21
  48.8 3.6 %collective-permute-done.6 = bf16[4,256,128]{2,1,0:T(8,128)(2,1)S(1)} collective-permute-done((bf16[4,256,128]{2,1,0:T(8,128)(2,1)S(1)}, bf16[4,256,128]{2,1,0:T(8,128)(2,1)S(1)}, u32[]{:S(2)}, u32[]{:S(2)}) %collective-permute-start.6) | collective-permute-done | bytes 262176 | tf_op jit(solution)/shard_map/ppermute | solution.py:21
  52.6 3.5 %all-to-all-start.1 = ((bf16[128,2,1024]{2,0,1:T(8,128)(2,1)}), bf16[128,2,1024]{2,0,1:T(8,128)(2,1)S(1)}, u32[]{:S(2)}, u32[]{:S(2)}) async-start(bf16[128,2,1024]{2,0,1:T(8,128)(2,1)} %bitcast.65), calls=%async_computation.1 | async-start | bytes 1048576 | tf_op jit(solution)/shard_map/all_to_all | solution.py:96
  57.3 5.8 %all-to-all-done.1 = bf16[128,2,1024]{2,0,1:T(8,128)(2,1)S(1)} async-done(((bf16[128,2,1024]{2,0,1:T(8,128)(2,1)}), bf16[128,2,1024]{2,0,1:T(8,128)(2,1)S(1)}, u32[]{:S(2)}, u32[]{:S(2)}) %all-to-all-start.1) | async-done | bytes 524320 | tf_op jit(solution)/shard_map/all_to_all | solution.py:96
  63.9 29.8 %shard_map.76 = (bf16[256,1024]{1,0:T(8,128)(2,1)}, f32[2304,128]{1,0:T(8,128)}, f32[2304,128]{1,0:T(8,128)}) custom-call(bf16[256,1024]{1,0:T(8,128)(2,1)} %bitcast.68, bf16[256,1024]{1,0:T(8,128)(2,1)} %bitcast.69, bf16[2304,128]{1,0:T(8,128)(2,1)} %bitcast.83, bf16[2304,128]{1,0:T(8,128)(2,1)} %bitcast.82, s32[1,256]{1,0:T(1,128)} %bitcast.90), custom_call_target="tpu_custom_call" | custom-call | tf_op jit(solution)/shard_map/pallas_call | solution.py:75
  93.7 2.5 %fusion.6 = (f32[1024,128]{1,0:T(8,128)S(1)}, f32[1024,128]{1,0:T(8,128)S(1)}, f32[1024,128]{1,0:T(8,128)S(1)}, f32[1024,128]{1,0:T(8,128)}) fusion(f32[2304,128]{1,0:T(8,128)} %get-tuple-element.8, f32[2304,128]{1,0:T(8,128)} %get-tuple-element.7), kind=kLoop, calls=%fused_computation.31 | loop fusion | bytes 4194304 | tf_op jit(solution)/shard_map/slice | solution.py:143
  98.7 3.5 %all-to-all-start.4 = ((bf16[2,128,1024]{2,1,0:T(8,128)(2,1)}), bf16[2,128,1024]{2,1,0:T(8,128)(2,1)S(1)}, u32[]{:S(2)}, u32[]{:S(2)}) async-start(bf16[2,128,1024]{2,1,0:T(8,128)(2,1)} %bitcast.19), calls=%async_computation.4 | async-start | bytes 1048576 | tf_op jit(solution)/shard_map/all_to_all | solution.py:154
  102.2 11.0 %collective-permute-done.12 = f32[4,256,128]{2,1,0:T(8,128)S(1)} collective-permute-done((f32[4,256,128]{2,1,0:T(8,128)S(1)}, f32[4,256,128]{2,1,0:T(8,128)S(1)}, u32[]{:S(2)}, u32[]{:S(2)}) %collective-permute-start.12) | collective-permute-done | bytes 524320 | tf_op jit(solution)/shard_map/ppermute | solution.py:21
  114.7 9.9 %collective-permute-done.8 = f32[4,256,128]{2,1,0:T(8,128)S(1)} collective-permute-done((f32[4,256,128]{2,1,0:T(8,128)}, f32[4,256,128]{2,1,0:T(8,128)S(1)}, u32[]{:S(2)}, u32[]{:S(2)}) %collective-permute-start.8) | collective-permute-done | bytes 524320 | tf_op jit(solution)/shard_map/ppermute | solution.py:21
  134.2 4.8 %collective-permute-done.15 = bf16[256,128]{1,0:T(8,128)(2,1)S(1)} collective-permute-done((bf16[256,128]{1,0:T(8,128)(2,1)S(1)}, bf16[256,128]{1,0:T(8,128)(2,1)S(1)}, u32[]{:S(2)}, u32[]{:S(2)}) %collective-permute-start.15) | collective-permute-done | bytes 65568 | tf_op jit(solution)/shard_map/ppermute | solution.py:21
  139.7 3.3 %all-to-all-start.6 = ((bf16[2,128,128]{2,1,0:T(8,128)(2,1)}), bf16[2,128,128]{2,1,0:T(8,128)(2,1)S(1)}, u32[]{:S(2)}, u32[]{:S(2)}) async-start(bf16[2,128,128]{2,1,0:T(8,128)(2,1)} %bitcast.29), calls=%async_computation.6 | async-start | bytes 131072 | tf_op jit(solution)/shard_map/all_to_all | solution.py:156
  143.7 3.4 %all-to-all-done.6 = bf16[2,128,128]{2,1,0:T(8,128)(2,1)S(1)} async-done(((bf16[2,128,128]{2,1,0:T(8,128)(2,1)}), bf16[2,128,128]{2,1,0:T(8,128)(2,1)S(1)}, u32[]{:S(2)}, u32[]{:S(2)}) %all-to-all-start.6) | async-done | bytes 65568 | tf_op jit(solution)/shard_map/all_to_all | solution.py:156
  147.1 3.3 %all-to-all-start.5 = ((bf16[2,128,128]{2,1,0:T(8,128)(2,1)}), bf16[2,128,128]{2,1,0:T(8,128)(2,1)S(1)}, u32[]{:S(2)}, u32[]{:S(2)}) async-start(bf16[2,128,128]{2,1,0:T(8,128)(2,1)} %bitcast.24), calls=%async_computation.5 | async-start | bytes 131072 | tf_op jit(solution)/shard_map/all_to_all | solution.py:155
  151.1 3.5 %all-to-all-done.5 = bf16[2,128,128]{2,1,0:T(8,128)(2,1)S(1)} async-done(((bf16[2,128,128]{2,1,0:T(8,128)(2,1)}), bf16[2,128,128]{2,1,0:T(8,128)(2,1)S(1)}, u32[]{:S(2)}, u32[]{:S(2)}) %all-to-all-start.5) | async-done | bytes 65568 | tf_op jit(solution)/shard_map/all_to_all | solution.py:155
  (71 shorter events, 27.0 us)
Async XLA Ops:
  0.6 13.4 %copy-start.4 = (bf16[128,2048]{1,0:T(8,128)(2,1)S(1)}, bf16[128,2048]{1,0:T(8,128)(2,1)}, u32[]{:S(2)}) copy-start(bf16[128,2048]{1,0:T(8,128)(2,1)} %param.8) | copy-start | bytes 1572868
  2.4 12.4 %all-to-all-start.3 = ((bf16[128,2,128]{2,0,1:T(8,128)(2,1)}), bf16[128,2,128]{2,0,1:T(8,128)(2,1)S(1)}, u32[]{:S(2)}, u32[]{:S(2)}) async-start(bf16[128,2,128]{2,0,1:T(8,128)(2,1)} %copy.36), calls=%async_computation.3 | async-start | bytes 131072 | tf_op jit(solution)/shard_map/all_to_all | solution.py:98
  14.8 10.3 %all-to-all-start.2 = ((bf16[128,2,128]{2,0,1:T(8,128)(2,1)}), bf16[128,2,128]{2,0,1:T(8,128)(2,1)S(1)}, u32[]{:S(2)}, u32[]{:S(2)}) async-start(bf16[128,2,128]{2,0,1:T(8,128)(2,1)} %copy.34), calls=%async_computation.2 | async-start | bytes 131072 | tf_op jit(solution)/shard_map/all_to_all | solution.py:97
  18.1 15.1 %collective-permute-start.4 = (bf16[1,256,128]{2,1,0:T(8,128)(2,1)S(1)}, bf16[1,256,128]{2,1,0:T(8,128)(2,1)S(1)}, u32[]{:S(2)}, u32[]{:S(2)}) collective-permute-start(bf16[1,256,128]{2,1,0:T(8,128)(2,1)S(1)} %bitcast.72), channel_id=1, source_target_pairs={{0,2},{2,4},{4,6},{6,8},{8,10},{10,12},{12,14},{14,16},{16,18},{18... | collective-permute-start | bytes 196616 | tf_op jit(solution)/shard_map/ppermute | solution.py:21
  19.6 32.9 %collective-permute-start.7 = (bf16[256,128]{1,0:T(8,128)(2,1)S(1)}, bf16[256,128]{1,0:T(8,128)(2,1)S(1)}, u32[]{:S(2)}, u32[]{:S(2)}) collective-permute-start(bf16[256,128]{1,0:T(8,128)(2,1)S(1)} %bitcast.74), channel_id=1, source_target_pairs={{0,16},{2,18},{4,20},{6,22},{8,24},{10,26},{12,28},{14,30},{1,17},... | collective-permute-start | bytes 196616 | tf_op jit(solution)/shard_map/ppermute | solution.py:21
  25.1 27.4 %all-to-all-start = ((bf16[128,2,1024]{2,0,1:T(8,128)(2,1)}), bf16[128,2,1024]{2,0,1:T(8,128)(2,1)S(1)}, u32[]{:S(2)}, u32[]{:S(2)}) async-start(bf16[128,2,1024]{2,0,1:T(8,128)(2,1)} %bitcast.66), calls=%async_computation | async-start | bytes 1048576 | tf_op jit(solution)/shard_map/all_to_all | solution.py:95
  28.6 28.6 %collective-permute-start.3 = (bf16[256,128]{1,0:T(8,128)(2,1)S(1)}, bf16[256,128]{1,0:T(8,128)(2,1)S(1)}, u32[]{:S(2)}, u32[]{:S(2)}) collective-permute-start(bf16[256,128]{1,0:T(8,128)(2,1)S(1)} %bitcast.77), channel_id=1, source_target_pairs={{0,16},{2,18},{4,20},{6,22},{8,24},{10,26},{12,28},{14,30},{1,17},... | collective-permute-start | bytes 196616 | tf_op jit(solution)/shard_map/ppermute | solution.py:21
  30.8 5.9 %collective-permute-start = (bf16[1,256,128]{2,1,0:T(8,128)(2,1)S(1)}, bf16[1,256,128]{2,1,0:T(8,128)(2,1)S(1)}, u32[]{:S(2)}, u32[]{:S(2)}) collective-permute-start(bf16[1,256,128]{2,1,0:T(8,128)(2,1)S(1)} %bitcast.78), channel_id=1, source_target_pairs={{0,2},{2,4},{4,6},{6,8},{8,10},{10,12},{12,14},{14,16},{16,18},{18... | collective-permute-start | bytes 196616 | tf_op jit(solution)/shard_map/ppermute | solution.py:21
  33.3 7.1 %collective-permute-start.5 = (bf16[2,256,128]{2,1,0:T(8,128)(2,1)S(1)}, bf16[2,256,128]{2,1,0:T(8,128)(2,1)S(1)}, u32[]{:S(2)}, u32[]{:S(2)}) collective-permute-start(bf16[2,256,128]{2,1,0:T(8,128)(2,1)S(1)} %pad_maximum_fusion.3), channel_id=1, source_target_pairs={{0,4},{2,6},{4,8},{6,10},{8,12},{10,14},{12,16},{14,18},{16,20},{1... | collective-permute-start | bytes 393224 | tf_op jit(solution)/shard_map/ppermute | solution.py:21
  36.7 9.1 %collective-permute-start.1 = (bf16[2,256,128]{2,1,0:T(8,128)(2,1)S(1)}, bf16[2,256,128]{2,1,0:T(8,128)(2,1)S(1)}, u32[]{:S(2)}, u32[]{:S(2)}) collective-permute-start(bf16[2,256,128]{2,1,0:T(8,128)(2,1)S(1)} %pad_maximum_fusion.2), channel_id=1, source_target_pairs={{0,4},{2,6},{4,8},{6,10},{8,12},{10,14},{12,16},{14,18},{16,20},{1... | collective-permute-start | bytes 393224 | tf_op jit(solution)/shard_map/ppermute | solution.py:21
  40.4 12.0 %collective-permute-start.6 = (bf16[4,256,128]{2,1,0:T(8,128)(2,1)S(1)}, bf16[4,256,128]{2,1,0:T(8,128)(2,1)S(1)}, u32[]{:S(2)}, u32[]{:S(2)}) collective-permute-start(bf16[4,256,128]{2,1,0:T(8,128)(2,1)S(1)} %pad_maximum_fusion.1), channel_id=1, source_target_pairs={{0,8},{2,10},{4,12},{6,14},{8,16},{10,18},{12,20},{14,22},{16,24},... | collective-permute-start | bytes 786440 | tf_op jit(solution)/shard_map/ppermute | solution.py:21
  45.8 11.4 %collective-permute-start.2 = (bf16[4,256,128]{2,1,0:T(8,128)(2,1)S(1)}, bf16[4,256,128]{2,1,0:T(8,128)(2,1)S(1)}, u32[]{:S(2)}, u32[]{:S(2)}) collective-permute-start(bf16[4,256,128]{2,1,0:T(8,128)(2,1)S(1)} %pad_maximum_fusion), channel_id=1, source_target_pairs={{0,8},{2,10},{4,12},{6,14},{8,16},{10,18},{12,20},{14,22},{16,24},... | collective-permute-start | bytes 786440 | tf_op jit(solution)/shard_map/ppermute | solution.py:21
  52.6 10.6 %all-to-all-start.1 = ((bf16[128,2,1024]{2,0,1:T(8,128)(2,1)}), bf16[128,2,1024]{2,0,1:T(8,128)(2,1)S(1)}, u32[]{:S(2)}, u32[]{:S(2)}) async-start(bf16[128,2,1024]{2,0,1:T(8,128)(2,1)} %bitcast.65), calls=%async_computation.1 | async-start | bytes 1048576 | tf_op jit(solution)/shard_map/all_to_all | solution.py:96
  96.1 17.1 %collective-permute-start.12 = (f32[4,256,128]{2,1,0:T(8,128)S(1)}, f32[4,256,128]{2,1,0:T(8,128)S(1)}, u32[]{:S(2)}, u32[]{:S(2)}) collective-permute-start(f32[4,256,128]{2,1,0:T(8,128)S(1)} %bitcast.87), channel_id=1, source_target_pairs={{8,0},{10,2},{12,4},{14,6},{16,8},{18,10},{20,12},{22,14},{24,16},... | collective-permute-start | bytes 1572872 | tf_op jit(solution)/shard_map/ppermute | solution.py:21
  97.4 27.1 %collective-permute-start.8 = (f32[4,256,128]{2,1,0:T(8,128)}, f32[4,256,128]{2,1,0:T(8,128)S(1)}, u32[]{:S(2)}, u32[]{:S(2)}) collective-permute-start(f32[4,256,128]{2,1,0:T(8,128)} %bitcast.22), channel_id=1, source_target_pairs={{8,0},{10,2},{12,4},{14,6},{16,8},{18,10},{20,12},{22,14},{24,16},... | collective-permute-start | bytes 1572872 | tf_op jit(solution)/shard_map/ppermute | solution.py:21
  98.7 31.6 %all-to-all-start.4 = ((bf16[2,128,1024]{2,1,0:T(8,128)(2,1)}), bf16[2,128,1024]{2,1,0:T(8,128)(2,1)S(1)}, u32[]{:S(2)}, u32[]{:S(2)}) async-start(bf16[2,128,1024]{2,1,0:T(8,128)(2,1)} %bitcast.19), calls=%async_computation.4 | async-start | bytes 1048576 | tf_op jit(solution)/shard_map/all_to_all | solution.py:154
  113.4 17.8 %collective-permute-start.13 = (f32[2,256,128]{2,1,0:T(8,128)S(1)}, f32[2,256,128]{2,1,0:T(8,128)S(1)}, u32[]{:S(2)}, u32[]{:S(2)}) collective-permute-start(f32[2,256,128]{2,1,0:T(8,128)S(1)} %slice.90), channel_id=1, source_target_pairs={{4,0},{6,2},{8,4},{10,6},{12,8},{14,10},{16,12},{18,14},{20,16},{2... | collective-permute-start | bytes 786440 | tf_op jit(solution)/shard_map/ppermute | solution.py:21
  124.6 8.3 %collective-permute-start.9 = (f32[2,256,128]{2,1,0:T(8,128)S(1)}, f32[2,256,128]{2,1,0:T(8,128)S(1)}, u32[]{:S(2)}, u32[]{:S(2)}) collective-permute-start(f32[2,256,128]{2,1,0:T(8,128)S(1)} %slice.85), channel_id=1, source_target_pairs={{4,0},{6,2},{8,4},{10,6},{12,8},{14,10},{16,12},{18,14},{20,16},{2... | collective-permute-start | bytes 786440 | tf_op jit(solution)/shard_map/ppermute | solution.py:21
  127.7 11.3 %collective-permute-start.15 = (bf16[256,128]{1,0:T(8,128)(2,1)S(1)}, bf16[256,128]{1,0:T(8,128)(2,1)S(1)}, u32[]{:S(2)}, u32[]{:S(2)}) collective-permute-start(bf16[256,128]{1,0:T(8,128)(2,1)S(1)} %slice.112), channel_id=1, source_target_pairs={{16,0},{18,2},{20,4},{22,6},{24,8},{26,10},{28,12},{30,14},{17,1},... | collective-permute-start | bytes 196616 | tf_op jit(solution)/shard_map/ppermute | solution.py:21
  129.0 14.0 %collective-permute-start.11 = (bf16[256,128]{1,0:T(8,128)(2,1)S(1)}, bf16[256,128]{1,0:T(8,128)(2,1)S(1)}, u32[]{:S(2)}, u32[]{:S(2)}) collective-permute-start(bf16[256,128]{1,0:T(8,128)(2,1)S(1)} %slice.113), channel_id=1, source_target_pairs={{16,0},{18,2},{20,4},{22,6},{24,8},{26,10},{28,12},{30,14},{17,1},... | collective-permute-start | bytes 196616 | tf_op jit(solution)/shard_map/ppermute | solution.py:21
  131.2 7.8 %collective-permute-start.14 = (f32[1,256,128]{2,1,0:T(8,128)S(1)}, f32[1,256,128]{2,1,0:T(8,128)S(1)}, u32[]{:S(2)}, u32[]{:S(2)}) collective-permute-start(f32[1,256,128]{2,1,0:T(8,128)S(1)} %slice.92), channel_id=1, source_target_pairs={{2,0},{4,2},{6,4},{8,6},{10,8},{12,10},{14,12},{16,14},{18,16},{20... | collective-permute-start | bytes 393224 | tf_op jit(solution)/shard_map/ppermute | solution.py:21
  132.9 10.1 %collective-permute-start.10 = (f32[1,256,128]{2,1,0:T(8,128)S(1)}, f32[1,256,128]{2,1,0:T(8,128)S(1)}, u32[]{:S(2)}, u32[]{:S(2)}) collective-permute-start(f32[1,256,128]{2,1,0:T(8,128)S(1)} %slice.87), channel_id=1, source_target_pairs={{2,0},{4,2},{6,4},{8,6},{10,8},{12,10},{14,12},{16,14},{18,16},{20... | collective-permute-start | bytes 393224 | tf_op jit(solution)/shard_map/ppermute | solution.py:21
  139.7 7.4 %all-to-all-start.6 = ((bf16[2,128,128]{2,1,0:T(8,128)(2,1)}), bf16[2,128,128]{2,1,0:T(8,128)(2,1)S(1)}, u32[]{:S(2)}, u32[]{:S(2)}) async-start(bf16[2,128,128]{2,1,0:T(8,128)(2,1)} %bitcast.29), calls=%async_computation.6 | async-start | bytes 131072 | tf_op jit(solution)/shard_map/all_to_all | solution.py:156
  147.1 7.4 %all-to-all-start.5 = ((bf16[2,128,128]{2,1,0:T(8,128)(2,1)}), bf16[2,128,128]{2,1,0:T(8,128)(2,1)S(1)}, u32[]{:S(2)}, u32[]{:S(2)}) async-start(bf16[2,128,128]{2,1,0:T(8,128)(2,1)} %bitcast.24), calls=%async_computation.5 | async-start | bytes 131072 | tf_op jit(solution)/shard_map/all_to_all | solution.py:155
  (4 other events, 27.8 us)

commit v2 on v1

v2 whole, which is shorter than its diff:
```python
import functools
import math

import jax
import jax.numpy as jnp
from jax import lax
from jax.experimental import pallas as pl
from jax.experimental.pallas import tpu as pltpu
from jax.sharding import PartitionSpec as P

SPAN = 8
PLANE = SPAN // 2
SLOTS = SPAN + PLANE

masked_score = -1e30
LOG2E = math.log2(math.e)
VMEM_LIMIT = 56 * 1024 * 1024
MESH = pl.DeviceIdType.MESH


def greet(partners):
    barrier = pltpu.get_barrier_semaphore()
    for partner in partners:
        pl.semaphore_signal(barrier, inc=1, device_id=partner, device_id_type=MESH)
    pl.semaphore_wait(barrier, len(partners))


def places():
    ctx, head = lax.axis_index("ctx"), lax.axis_index("head")
    count = lax.axis_size("ctx")
    slot = lax.rem(ctx, PLANE)
    base = ctx - slot
    up = lax.rem(ctx + PLANE, count)
    down = lax.rem(ctx + count - PLANE, count)
    far = lax.rem(slot + PLANE // 2, PLANE)
    near = slot + 1 - 2 * lax.rem(slot, 2)
    diagonal = lax.rem(near + PLANE // 2, PLANE)
    return ctx, head, slot, base, up, down, near, far, diagonal


def head_peers(head):
    count = lax.axis_size("head")
    return [lax.rem(head + step, count) for step in range(1, count)]


def rows_of(index, length):
    return pl.ds(pl.multiple_of(index * length, length), length)


def gather_kernel(
    query_ref, grad_ref, key_ref, value_ref, query_out, grad_out, key_out, value_out, local_sems, x_send, x_recv, c_send, c_recv
):
    ctx, head, slot, base, up, down, near, far, diagonal = places()
    peers = head_peers(head)
    tokens = key_ref.shape[0]
    length = tokens * lax.axis_size("head")
    pairs = [
        (key_ref, key_out, slot + SPAN),
        (value_ref, value_out, slot + SPAN),
        (query_ref, query_out, 0),
        (grad_ref, grad_out, 0),
    ]
    greet(
        [{"head": peer} for peer in peers]
        + [{"ctx": up}, {"ctx": down}, {"ctx": base + near}, {"ctx": base + far}]
    )
    x_copies = []
    for index, (source, target, block) in enumerate(pairs):
        width = target.shape[1]
        start = pl.multiple_of(block * length + head * tokens, tokens)
        copies = []
        for step, peer in enumerate(peers):
            copy = pltpu.make_async_remote_copy(
                src_ref=source.at[:, rows_of(peer, width)],
                dst_ref=target.at[pl.ds(start, tokens), :],
                send_sem=x_send.at[index, step],
                recv_sem=x_recv.at[index, step],
                device_id={"head": peer},
                device_id_type=MESH,
            )
            copy.start()
            copies.append(copy)
        local = pltpu.make_async_copy(
            source.at[:, rows_of(head, width)], target.at[pl.ds(start, tokens), :], local_sems.at[index]
        )
        local.start()
        x_copies.append((local, copies))

    def arrive(index):
        local, copies = x_copies[index]
        local.wait()
        for copy in copies:
            copy.wait_recv()

    def push(array, kind, level, block, partner):
        target = (key_out, value_out)[array]
        rows = rows_of((2 - level) * PLANE + block, length)
        copy = pltpu.make_async_remote_copy(
            src_ref=target.at[rows, :],
            dst_ref=target.at[rows, :]
            if kind
            else target.at[rows_of((1 - level) * PLANE + block, length), :],
            send_sem=c_send.at[array, kind, level],
            recv_sem=c_recv.at[array, kind, level],
            device_id={"ctx": partner},
            device_id_type=MESH,
        )
        copy.start()
        copies[array, kind, level] = copy

    copies = {}

    def spread(array, level):
        if level < 2:
            push(array, 0, level, slot, up)
        push(array, 1, level, slot, base + far)
        push(array, 2, level, slot, base + near)

    def relay(array, level):
        copies[array, 1, level].wait_recv()
        push(array, 3, level, far, base + near)

    for array in range(2):
        arrive(array)
        spread(array, 0)
    for array in range(2):
        copies[array, 0, 0].wait_recv()
        spread(array, 1)
    for array in range(2):
        relay(array, 0)
    for array in range(2):
        copies[array, 0, 1].wait_recv()
        spread(array, 2)
    for level in (1, 2):
        for array in range(2):
            relay(array, level)
    for array in range(2):
        for level in range(3):
            copies[array, 2, level].wait_recv()
            copies[array, 3, level].wait_recv()
    arrive(2)
    arrive(3)
    for _, remote in x_copies:
        for copy in remote:
            copy.wait_send()
    for copy in copies.values():
        copy.wait_send()


def gather(queries, output_cotangent, keys, values):
    heads = lax.axis_size("head")
    tokens, width = queries.shape
    length = tokens * heads
    head_width = keys.shape[1] // heads
    vmem = pl.BlockSpec(memory_space=pltpu.VMEM)
    rows = jax.ShapeDtypeStruct((length, width // heads), jnp.bfloat16)
    window = jax.ShapeDtypeStruct((SLOTS * length, head_width), jnp.bfloat16)
    dma = pltpu.SemaphoreType.DMA
    return pl.pallas_call(
        gather_kernel,
        out_shape=(rows, rows, window, window),
        in_specs=[vmem] * 4,
        out_specs=(vmem,) * 4,
        scratch_shapes=[dma((4,)), dma((4, heads)), dma((4, heads)), dma((2, 4, 3)), dma((2, 4, 3))],
        compiler_params=pltpu.CompilerParams(
            collective_id=0, has_side_effects=True, vmem_limit_bytes=VMEM_LIMIT
        ),
    )(queries, output_cotangent, keys, values)


def attention_kernel(
    query_ref, grad_ref, key_ref, value_ref, bound_ref, dq_ref, dk_ref, dv_ref,
    bias_ref, key_t_ref, value_t_ref, key_sum, value_sum, *, scaling
):
    length = query_ref.shape[0]
    width = key_ref.shape[1]
    window = key_sum.shape[0]
    group_size = query_ref.shape[1] // width
    own_block = lax.axis_index("ctx")
    slot = lax.rem(own_block, PLANE)
    reach = pl.ds(pl.multiple_of(slot * length, length), window)
    key_pos = (own_block - SPAN) * length + lax.broadcasted_iota(jnp.int32, (window, length), 0)
    query_pos = own_block * length + lax.broadcasted_iota(jnp.int32, (1, length), 1)
    allowed = (key_pos >= bound_ref[...]) & (key_pos <= query_pos)
    bias_ref[...] = jnp.where(allowed, 0.0, masked_score)
    key_t_ref[...] = key_ref[reach, :].T
    value_t_ref[...] = value_ref[reach, :].T
    key_sum[...] = jnp.zeros_like(key_sum)
    value_sum[...] = jnp.zeros_like(value_sum)
    contract_last = (((1,), (1,)), ((), ()))

    @pl.loop(0, group_size)
    def _(g):
        cols = pl.ds(pl.multiple_of(g * width, width), width)
        query = query_ref[:, cols]
        grad = grad_ref[:, cols]
        scores = lax.dot_general(key_ref[reach, :], query, contract_last, preferred_element_type=jnp.float32)
        scores = scores * (scaling * LOG2E) + bias_ref[...]
        powers = jnp.exp2(scores - jnp.max(scores, axis=0, keepdims=True))
        weights = powers * (1.0 / jnp.sum(powers, axis=0, keepdims=True))
        rounded = weights.astype(jnp.bfloat16)
        out_t = jnp.dot(value_t_ref[...], rounded, preferred_element_type=jnp.float32)
        row_dot = jnp.sum(grad.astype(jnp.float32).T * out_t, axis=0, keepdims=True)
        grad_weights = lax.dot_general(value_ref[reach, :], grad, contract_last, preferred_element_type=jnp.float32)
        grad_scores = (weights * (grad_weights - row_dot)).astype(jnp.bfloat16)
        dq_t = jnp.dot(key_t_ref[...], grad_scores, preferred_element_type=jnp.float32)
        dq_ref[:, cols] = (dq_t * scaling).T.astype(jnp.bfloat16)
        key_sum[...] += jnp.dot(grad_scores, query, preferred_element_type=jnp.float32)
        value_sum[...] += jnp.dot(rounded, grad, preferred_element_type=jnp.float32)

    dk_ref[...] = jnp.zeros_like(dk_ref)
    dv_ref[...] = jnp.zeros_like(dv_ref)
    dk_ref[reach, :] = (key_sum[...] * scaling).astype(jnp.bfloat16)
    dv_ref[reach, :] = value_sum[...].astype(jnp.bfloat16)


def attention(query_rows, grad_rows, key_window, value_window, bound):
    length = query_rows.shape[0]
    width = key_window.shape[1]
    window = (SPAN + 1) * length
    vmem = pl.BlockSpec(memory_space=pltpu.VMEM)
    parts = jax.ShapeDtypeStruct(key_window.shape, jnp.bfloat16)
    return pl.pallas_call(
        functools.partial(attention_kernel, scaling=width ** (-0.5)),
        out_shape=(jax.ShapeDtypeStruct(query_rows.shape, jnp.bfloat16), parts, parts),
        in_specs=[vmem] * 5,
        out_specs=(vmem,) * 3,
        scratch_shapes=[
            pltpu.VMEM((window, length), jnp.float32),
            pltpu.VMEM((width, window), jnp.bfloat16),
            pltpu.VMEM((width, window), jnp.bfloat16),
            pltpu.VMEM((window, width), jnp.float32),
            pltpu.VMEM((window, width), jnp.float32),
        ],
        compiler_params=pltpu.CompilerParams(vmem_limit_bytes=VMEM_LIMIT),
    )(query_rows, grad_rows, key_window, value_window, bound)


def reduce_kernel(
    dq_ref, dk_ref, dv_ref, dq_out, dk_out, dv_out,
    near_buf, own_sum, far_sum, far_buf, down_src, down_buf, final,
    local_sems, x_send, x_recv, c_send, c_recv
):
    ctx, head, slot, base, up, down, near, far, diagonal = places()
    peers = head_peers(head)
    tokens = dq_out.shape[0]
    length = dq_ref.shape[0]
    parts = (dk_ref, dv_ref)
    greet(
        [{"head": peer} for peer in peers]
        + [{"ctx": up}, {"ctx": down}, {"ctx": base + near}, {"ctx": base + far}]
    )
    waits = []

    def exchange(index, source, target):
        width = source.shape[1]
        copies = []
        for step, peer in enumerate(peers):
            copy = pltpu.make_async_remote_copy(
                src_ref=source.at[rows_of(peer, tokens), :],
                dst_ref=target.at[:, rows_of(head, width)],
                send_sem=x_send.at[index, step],
                recv_sem=x_recv.at[index, step],
                device_id={"head": peer},
                device_id_type=MESH,
            )
            copy.start()
            copies.append(copy)
        local = pltpu.make_async_copy(
            source.at[rows_of(head, tokens), :], target.at[:, rows_of(head, width)], local_sems.at[index]
        )
        local.start()
        waits.append((local, copies))

    copies = {}

    def push(array, kind, level, source, target, partner):
        copy = pltpu.make_async_remote_copy(
            src_ref=source,
            dst_ref=target,
            send_sem=c_send.at[array, kind, level],
            recv_sem=c_recv.at[array, kind, level],
            device_id={"ctx": partner},
            device_id_type=MESH,
        )
        copy.start()
        copies[array, kind, level] = copy

    def block(level, position):
        return rows_of((2 - level) * PLANE + position, length)

    for level in (2, 1, 0):
        for array in range(2):
            part = parts[array]
            push(array, 0, level, part.at[block(level, diagonal), :], near_buf.at[array, level, 0], base + near)
            push(array, 1, level, part.at[block(level, near), :], near_buf.at[array, level, 1], base + near)
    exchange(0, dq_ref, dq_out)
    for level in (2, 1, 0):
        for array in range(2):
            part = parts[array]
            copies[array, 0, level].wait_recv()
            far_sum[array, level] = (
                part[block(level, far), :].astype(jnp.float32) + near_buf[array, level, 0].astype(jnp.float32)
            ).astype(jnp.bfloat16)
            push(array, 2, level, far_sum.at[array, level], far_buf.at[array, level], base + far)
    for level in (2, 1, 0):
        for array in range(2):
            part = parts[array]
            copies[array, 1, level].wait_recv()
            own_sum[array, level] = part[block(level, slot), :].astype(jnp.float32) + near_buf[
                array, level, 1
            ].astype(jnp.float32)
    for level in (2, 1, 0):
        for array in range(2):
            copies[array, 2, level].wait_recv()
            total = own_sum[array, level] + far_buf[array, level].astype(jnp.float32)
            if level < 2:
                copies[array, 3, level + 1].wait_recv()
                total = total + down_buf[array, level].astype(jnp.float32)
            if level > 0:
                down_src[array, level - 1] = total.astype(jnp.bfloat16)
                push(array, 3, level, down_src.at[array, level - 1], down_buf.at[array, level - 1], down)
            else:
                final[array] = total.astype(jnp.bfloat16)
                exchange(1 + array, final.at[array], (dk_out, dv_out)[array])
    for local, remote in waits:
        local.wait()
        for copy in remote:
            copy.wait()
    for copy in copies.values():
        copy.wait_send()


def reduce(grad_query, part_keys, part_values):
    heads = lax.axis_size("head")
    length, width = grad_query.shape
    head_width = part_keys.shape[1]
    tokens = length // heads
    vmem = pl.BlockSpec(memory_space=pltpu.VMEM)
    dma = pltpu.SemaphoreType.DMA
    block = (length, head_width)
    narrow = jax.ShapeDtypeStruct((tokens, head_width * heads), jnp.bfloat16)
    return pl.pallas_call(
        reduce_kernel,
        out_shape=(jax.ShapeDtypeStruct((tokens, width * heads), jnp.bfloat16), narrow, narrow),
        in_specs=[vmem] * 3,
        out_specs=(vmem,) * 3,
        scratch_shapes=[
            pltpu.VMEM((2, 3, 2) + block, jnp.bfloat16),
            pltpu.VMEM((2, 3) + block, jnp.float32),
            pltpu.VMEM((2, 3) + block, jnp.bfloat16),
            pltpu.VMEM((2, 3) + block, jnp.bfloat16),
            pltpu.VMEM((2, 2) + block, jnp.bfloat16),
            pltpu.VMEM((2, 2) + block, jnp.bfloat16),
            pltpu.VMEM((2,) + block, jnp.bfloat16),
            dma((3,)), dma((3, heads)), dma((3, heads)), dma((2, 4, 3)), dma((2, 4, 3)),
        ],
        compiler_params=pltpu.CompilerParams(
            collective_id=1, has_side_effects=True, vmem_limit_bytes=VMEM_LIMIT
        ),
    )(grad_query, part_keys, part_values)


def on_device(queries, keys, values, output_cotangent, doc_ids):
    query_rows, grad_rows, key_window, value_window = gather(queries, output_cotangent, keys, values)
    length = query_rows.shape[0]
    own_docs = lax.dynamic_slice_in_dim(doc_ids, lax.axis_index("ctx") * length, length, 0)
    bound = jnp.sum((doc_ids[:, None] < own_docs[None, :]).astype(jnp.int32), axis=0)[None]
    return reduce(*attention(query_rows, grad_rows, key_window, value_window, bound))


def solution(mesh):
    rows = P(("ctx", "head"), None)
    return jax.shard_map(
        on_device,
        mesh=mesh,
        in_specs=(rows, rows, rows, rows, P()),
        out_specs=(rows, rows, rows),
        check_vma=False,
    )
```

time: 157 us -> 82.2 us (0.52)
  starting transfers between devices: 61.6 us -> 0 us
  Pallas kernels: 29.8 us -> 74.2 us
  waiting for transfers between devices: 43.8 us -> 0 us
  local copies, waits for them, and re-layouts: 14.3 us -> 3.95 us
    pallas_call x0 -> x2, Pallas kernels: none -> 44.7 us  [the longest x1 25.1 us: gather(): pl.pallas_call(gather_kernel, out_shape=(rows, rows, window, window), in_...]
    ppermute x16 -> x0, starting transfers between devices: 37 us -> none  [shifted(): lax.ppermute(value, axis, [(source, source + steps) for source in range(l...]
    ppermute x16 -> x0, waiting for transfers between devices: 31.1 us -> none  [shifted(): lax.ppermute(value, axis, [(source, source + steps) for source in range(l...]
    all_to_all x7 -> x0, starting transfers between devices: 24.6 us -> none  [the longest x1 4.23 us: on_device(): lax.all_to_all(values, 'head', split_axis=1, concat_axis=0, tiled=True)]
    all_to_all x7 -> x0, waiting for transfers between devices: 12.7 us -> none  [the longest x1 5.82 us: on_device(): lax.all_to_all(output_cotangent, 'head', split_axis=1, concat_axis=0, til...]
    all_to_all x7 -> x0, local copies, waits for them, and re-layouts: 6.31 us -> none  [the longest x1 1.87 us: on_device(): lax.all_to_all(queries, 'head', split_axis=1, concat_axis=0, tiled=True)]
    slice x7 -> x0, local copies, waits for them, and re-layouts: 4.35 us -> none  [the longest x3 2.49 us: on_device(): stacked_values[stride:2 * stride]]
    unnamed x20 -> x7, local copies, waits for them, and re-layouts: 2.89 us -> 3.18 us
  transfers between devices with their start and end apart: 23 -> 0, of which waited for: 10 -> 0; matrix products, arithmetic and copies ran while one was open for 9% -> 0% of each run, Pallas kernels for 0% -> 0%
where the time goes in v2:
time: 82.2 us; the launch traced here: 81.8 us
  Pallas kernels  74.2 us (90%)
  local copies, waits for them, and re-layouts  3.95 us (5%)
  other arithmetic  3.03 us (4%)
    pallas_call x1, Pallas kernels, attention(): pl.pallas_call(functools.partial(attention_kernel, scaling=width ** (-0.5...  29.5 us
    pallas_call x1, Pallas kernels, gather(): pl.pallas_call(gather_kernel, out_shape=(rows, rows, window, window), in_...  25.1 us
    pallas_call x1, Pallas kernels, reduce(): pl.pallas_call(reduce_kernel, out_shape=(jax.ShapeDtypeStruct((tokens, wi...  19.5 us
    unnamed x7, local copies, waits for them, and re-layouts  3.18 us
    reduce_sum x1, other arithmetic, on_device(): jnp.sum((doc_ids[:, None] < own_docs[None, :]).astype(jnp.int32), axis=0)  3.03 us

profile of v2, /device:TPU:0, one launch (start us, length us, event | category | flops | bytes accessed | tf_op | source)
XLA Modules:
  0.0 81.8 jit_solution(10533370591634981710)
XLA Ops:
  0.6 0.8 dynamic_slice.3
  1.4 3.0 %convert_reduce_fusion = s32[256]{0:T(256)} fusion(s32[256]{0:T(256)S(1)} %dynamic_slice.3, s32[4096]{0:T(1024)} %param.9), kind=kLoop, calls=%fused_computation | loop fusion | flops 3145472 | bytes 18432 | tf_op jit(solution)/shard_map/reduce_sum | solution.py:368
  4.4 25.1 %shard_map.76 = (bf16[256,1024]{1,0:T(8,128)(2,1)}, bf16[256,1024]{1,0:T(8,128)(2,1)}, bf16[3072,128]{1,0:T(8,128)(2,1)}, bf16[3072,128]{1,0:T(8,128)(2,1)}) custom-call(bf16[128,2048]{1,0:T(8,128)(2,1)} %query_ref.1, bf16[128,2048]{1,0:T(8,128)(2,1)} %grad_ref.1, bf16[128,256]{1,0:T(8,128)(2,1)} %key_ref.1, bf16[128,256]{1,0:T(8,128)(2,1)} %value_ref.1), custom_call_target="tpu_custom_call" | custom-call | tf_op jit(solution)/shard_map/pallas_call | solution.py:159
  29.6 29.5 %shard_map.77 = (bf16[256,1024]{1,0:T(8,128)(2,1)}, bf16[3072,128]{1,0:T(8,128)(2,1)}, bf16[3072,128]{1,0:T(8,128)(2,1)}) custom-call(bf16[256,1024]{1,0:T(8,128)(2,1)} %get-tuple-element.10.query_ref, bf16[256,1024]{1,0:T(8,128)(2,1)} %get-tuple-element.11.grad_ref, bf16[3072,128]{1,0:T(8,128)(2,1)} %get-tuple-element.12.key_ref, ...), custom_call_target="tpu_custom_call" | custom-call | tf_op jit(solution)/shard_map/pallas_call | solution.py:223
  59.1 19.5 %shard_map.78 = (bf16[128,2048]{1,0:T(8,128)(2,1)}, bf16[128,256]{1,0:T(8,128)(2,1)}, bf16[128,256]{1,0:T(8,128)(2,1)}) custom-call(bf16[256,1024]{1,0:T(8,128)(2,1)} %get-tuple-element.14.dq_ref, bf16[3072,128]{1,0:T(8,128)(2,1)} %get-tuple-element.15.dk_ref, bf16[3072,128]{1,0:T(8,128)(2,1)} %get-tuple-element.16.dv_ref), custom_call_target="tpu_custom_call" | custom-call | tf_op jit(solution)/shard_map/pallas_call | solution.py:343
  78.6 0.0 copy-start.1
  78.6 0.0 copy-start
  78.6 1.9 %copy.11 = bf16[128,2048]{1,0:T(8,128)(2,1)} copy(bf16[128,2048]{1,0:T(8,128)(2,1)} %get-tuple-element.20) | data formatting | bytes 1048576
  80.6 0.0 copy-done.1
  80.6 0.6 copy.12
  81.2 0.0 copy-done
  81.2 0.6 copy.13
Async XLA Ops:
  78.6 1.9 %copy-start.1 = (bf16[128,256]{1,0:T(8,128)(2,1)S(1)}, bf16[128,256]{1,0:T(8,128)(2,1)}, u32[]{:S(2)}) copy-start(bf16[128,256]{1,0:T(8,128)(2,1)} %get-tuple-element.21) | copy-start | bytes 196612
  78.6 2.6 %copy-start = (bf16[128,256]{1,0:T(8,128)(2,1)S(1)}, bf16[128,256]{1,0:T(8,128)(2,1)}, u32[]{:S(2)}) copy-start(bf16[128,256]{1,0:T(8,128)(2,1)} %get-tuple-element.22) | copy-start | bytes 196612

commit v3 on v2

--- a/solution.py
+++ b/solution.py
@@ -86,65 +86,95 @@
         local.start()
         x_copies.append((local, copies))
 
-    def arrive(index):
-        local, copies = x_copies[index]
-        local.wait()
-        for copy in copies:
-            copy.wait_recv()
-
-    def push(array, kind, level, block, partner):
+    def arrive_local(index):
+        x_copies[index][0].wait()
+
+    plane = ctx // PLANE
+    last = lax.axis_size("ctx") // PLANE - 1
+    order = [head] + [lax.rem(head + len(peers) + 1 - step, len(peers) + 1) for step in range(1, len(peers) + 1)]
+
+    def copy_of(array, piece, kind, level):
         target = (key_out, value_out)[array]
-        rows = rows_of((2 - level) * PLANE + block, length)
-        copy = pltpu.make_async_remote_copy(
-            src_ref=target.at[rows, :],
-            dst_ref=target.at[rows, :]
-            if kind
-            else target.at[rows_of((1 - level) * PLANE + block, length), :],
-            send_sem=c_send.at[array, kind, level],
-            recv_sem=c_recv.at[array, kind, level],
+        block, shift, partner = (
+            (slot, 1, up), (slot, 0, base + far), (slot, 0, base + near), (far, 0, base + near)
+        )[kind]
+        offset = block * length + order[piece] * tokens
+        source = pl.ds(pl.multiple_of((2 - level) * PLANE * length + offset, tokens), tokens)
+        landing = pl.ds(pl.multiple_of((2 - level - shift) * PLANE * length + offset, tokens), tokens)
+        return pltpu.make_async_remote_copy(
+            src_ref=target.at[source, :],
+            dst_ref=target.at[landing, :],
+            send_sem=c_send.at[array, piece, kind, level],
+            recv_sem=c_recv.at[array, piece, kind, level],
             device_id={"ctx": partner},
             device_id_type=MESH,
         )
-        copy.start()
-        copies[array, kind, level] = copy
-
-    copies = {}
-
-    def spread(array, level):
+
+    def spread(array, piece, level):
         if level < 2:
-            push(array, 0, level, slot, up)
-        push(array, 1, level, slot, base + far)
-        push(array, 2, level, slot, base + near)
-
-    def relay(array, level):
-        copies[array, 1, level].wait_recv()
-        push(array, 3, level, far, base + near)
-
-    for array in range(2):
-        arrive(array)
-        spread(array, 0)
-    for array in range(2):
-        copies[array, 0, 0].wait_recv()
-        spread(array, 1)
-    for array in range(2):
-        relay(array, 0)
-    for array in range(2):
-        copies[array, 0, 1].wait_recv()
-        spread(array, 2)
+            @pl.when(plane < last)
+            def _():
+                copy_of(array, piece, 0, level).start()
+
+        copy_of(array, piece, 1, level).start()
+        copy_of(array, piece, 2, level).start()
+
+    def relay(array, piece, level):
+        copy_of(array, piece, 1, level).wait_recv()
+        copy_of(array, piece, 3, level).start()
+
+    pieces = range(len(order))
+    for piece in pieces:
+        for array in range(2):
+            if piece == 0:
+                arrive_local(array)
+            else:
+                x_copies[array][1][piece - 1].wait_recv()
+            spread(array, piece, 0)
     for level in (1, 2):
-        for array in range(2):
-            relay(array, level)
-    for array in range(2):
-        for level in range(3):
-            copies[array, 2, level].wait_recv()
-            copies[array, 3, level].wait_recv()
-    arrive(2)
-    arrive(3)
-    for _, remote in x_copies:
+        for piece in pieces:
+            @pl.when(plane >= level)
+            def _():
+                for array in range(2):
+                    copy_of(array, piece, 0, level - 1).wait_recv()
+                    spread(array, piece, level)
+
+            for array in range(2):
+                if level == 1:
+                    relay(array, piece, 0)
+                else:
+                    @pl.when(plane >= 1)
+                    def _():
+                        relay(array, piece, 1)
+
+    @pl.when(plane >= 2)
+    def _():
+        for piece in pieces:
+            for array in range(2):
+                relay(array, piece, 2)
+
+    for level in range(3):
+        @pl.when(plane >= level)
+        def _():
+            for piece in pieces:
+                for array in range(2):
+                    copy_of(array, piece, 1, level).wait_send()
+                    copy_of(array, piece, 2, level).wait()
+                    copy_of(array, piece, 3, level).wait()
+            if level < 2:
+                @pl.when(plane < last)
+                def _():
+                    for piece in pieces:
+                        for array in range(2):
+                            copy_of(array, piece, 0, level).wait_send()
+
+    for index, (local, remote) in enumerate(x_copies):
+        if index >= 2:
+            local.wait()
+            for copy in remote:
+                copy.wait_recv()
         for copy in remote:
             copy.wait_send()
-    for copy in copies.values():
-        copy.wait_send()
 
 
 def gather(queries, output_cotangent, keys, values):
@@ -161,7 +191,7 @@
         out_shape=(rows, rows, window, window),
         in_specs=[vmem] * 4,
         out_specs=(vmem,) * 4,
-        scratch_shapes=[dma((4,)), dma((4, heads)), dma((4, heads)), dma((2, 4, 3)), dma((2, 4, 3))],
+        scratch_shapes=[dma((4,)), dma((4, heads)), dma((4, heads)), dma((2, heads, 4, 3)), dma((2, heads, 4, 3))],
         compiler_params=pltpu.CompilerParams(
             collective_id=0, has_side_effects=True, vmem_limit_bytes=VMEM_LIMIT
         ),
@@ -169,8 +199,8 @@
 
 
 def attention_kernel(
-    query_ref, grad_ref, key_ref, value_ref, bound_ref, dq_ref, dk_ref, dv_ref,
-    bias_ref, key_t_ref, value_t_ref, key_sum, value_sum, *, scaling
+    query_ref, grad_ref, key_ref, value_ref, doc_ref, dq_ref, dk_ref, dv_ref,
+    bias_ref, key_win, value_win, key_t_ref, value_t_ref, key_sum, value_sum, *, scaling
 ):
     length = query_ref.shape[0]
     width = key_ref.shape[1]
@@ -179,12 +209,25 @@
     own_block = lax.axis_index("ctx")
     slot = lax.rem(own_block, PLANE)
     reach = pl.ds(pl.multiple_of(slot * length, length), window)
-    key_pos = (own_block - SPAN) * length + lax.broadcasted_iota(jnp.int32, (window, length), 0)
-    query_pos = own_block * length + lax.broadcasted_iota(jnp.int32, (1, length), 1)
-    allowed = (key_pos >= bound_ref[...]) & (key_pos <= query_pos)
-    bias_ref[...] = jnp.where(allowed, 0.0, masked_score)
-    key_t_ref[...] = key_ref[reach, :].T
-    value_t_ref[...] = value_ref[reach, :].T
+    first_key = (own_block - SPAN) * length
+    lanes = doc_ref.shape[1]
+    own_row = own_block * (length // lanes)
+    query_docs = jnp.concatenate(
+        [doc_ref[pl.ds(own_row + i, 1), :] for i in range(length // lanes)], axis=1
+    )
+    query_pos = own_block * length + lax.broadcasted_iota(jnp.int32, (lanes, length), 1)
+    for i in range(window // lanes):
+        row = jnp.maximum((own_block - SPAN) * (length // lanes) + i, 0)
+        key_docs = jnp.broadcast_to(doc_ref[pl.ds(row, 1), :], (lanes, lanes)).T
+        key_docs = jnp.concatenate([key_docs] * (length // lanes), axis=1)
+        key_pos = first_key + i * lanes + lax.broadcasted_iota(jnp.int32, (lanes, length), 0)
+        allowed = (key_docs == query_docs) & (key_pos <= query_pos) & (key_pos >= 0)
+        bias_ref[i * lanes : (i + 1) * lanes, :] = jnp.where(allowed, 0.0, masked_score)
+    present = first_key + lax.broadcasted_iota(jnp.int32, (window, width), 0) >= 0
+    key_win[...] = jnp.where(present, key_ref[reach, :].astype(jnp.float32), 0.0).astype(jnp.bfloat16)
+    value_win[...] = jnp.where(present, value_ref[reach, :].astype(jnp.float32), 0.0).astype(jnp.bfloat16)
+    key_t_ref[...] = key_win[...].T
+    value_t_ref[...] = value_win[...].T
     key_sum[...] = jnp.zeros_like(key_sum)
     value_sum[...] = jnp.zeros_like(value_sum)
     contract_last = (((1,), (1,)), ((), ()))
@@ -194,14 +237,14 @@
         cols = pl.ds(pl.multiple_of(g * width, width), width)
         query = query_ref[:, cols]
         grad = grad_ref[:, cols]
-        scores = lax.dot_general(key_ref[reach, :], query, contract_last, preferred_element_type=jnp.float32)
+        scores = lax.dot_general(key_win[...], query, contract_last, preferred_element_type=jnp.float32)
         scores = scores * (scaling * LOG2E) + bias_ref[...]
         powers = jnp.exp2(scores - jnp.max(scores, axis=0, keepdims=True))
         weights = powers * (1.0 / jnp.sum(powers, axis=0, keepdims=True))
         rounded = weights.astype(jnp.bfloat16)
         out_t = jnp.dot(value_t_ref[...], rounded, preferred_element_type=jnp.float32)
         row_dot = jnp.sum(grad.astype(jnp.float32).T * out_t, axis=0, keepdims=True)
-        grad_weights = lax.dot_general(value_ref[reach, :], grad, contract_last, preferred_element_type=jnp.float32)
+        grad_weights = lax.dot_general(value_win[...], grad, contract_last, preferred_element_type=jnp.float32)
         grad_scores = (weights * (grad_weights - row_dot)).astype(jnp.bfloat16)
         dq_t = jnp.dot(key_t_ref[...], grad_scores, preferred_element_type=jnp.float32)
         dq_ref[:, cols] = (dq_t * scaling).T.astype(jnp.bfloat16)
@@ -214,7 +257,7 @@
     dv_ref[reach, :] = value_sum[...].astype(jnp.bfloat16)
 
 
-def attention(query_rows, grad_rows, key_window, value_window, bound):
+def attention(query_rows, grad_rows, key_window, value_window, docs):
     length = query_rows.shape[0]
     width = key_window.shape[1]
     window = (SPAN + 1) * length
@@ -227,13 +270,15 @@
         out_specs=(vmem,) * 3,
         scratch_shapes=[
             pltpu.VMEM((window, length), jnp.float32),
+            pltpu.VMEM((window, width), jnp.bfloat16),
+            pltpu.VMEM((window, width), jnp.bfloat16),
             pltpu.VMEM((width, window), jnp.bfloat16),
             pltpu.VMEM((width, window), jnp.bfloat16),
             pltpu.VMEM((window, width), jnp.float32),
             pltpu.VMEM((window, width), jnp.float32),
         ],
         compiler_params=pltpu.CompilerParams(vmem_limit_bytes=VMEM_LIMIT),
-    )(query_rows, grad_rows, key_window, value_window, bound)
+    )(query_rows, grad_rows, key_window, value_window, docs)
 
 
 def reduce_kernel(
@@ -272,63 +317,138 @@
         local.start()
         waits.append((local, copies))
 
-    copies = {}
-
-    def push(array, kind, level, source, target, partner):
-        copy = pltpu.make_async_remote_copy(
-            src_ref=source,
-            dst_ref=target,
-            send_sem=c_send.at[array, kind, level],
-            recv_sem=c_recv.at[array, kind, level],
-            device_id={"ctx": partner},
+    plane = ctx // PLANE
+    last = lax.axis_size("ctx") // PLANE - 1
+    order = peers + [head]
+    pieces = range(len(order))
+
+    def rows(level, position, piece):
+        start = ((2 - level) * PLANE + position) * length + order[piece] * tokens
+        return pl.ds(pl.multiple_of(start, tokens), tokens)
+
+    def slab(piece):
+        return pl.ds(pl.multiple_of(order[piece] * tokens, tokens), tokens)
+
+    def copy_of(array, piece, kind, level):
+        part = (dk_ref, dv_ref)[array]
+        here = slab(piece)
+        source, target, place = (
+            (lambda: part.at[rows(level, diagonal, piece), :], lambda: near_buf.at[array, level, 0, here], {"ctx": base + near}),
+            (lambda: part.at[rows(level, near, piece), :], lambda: near_buf.at[array, level, 1, here], {"ctx": base + near}),
+            (lambda: far_sum.at[array, level, here], lambda: far_buf.at[array, level, here], {"ctx": base + far}),
+            (lambda: down_src.at[array, level - 1, here], lambda: down_buf.at[array, level - 1, here], {"ctx": down}),
+        )[kind]
+        return pltpu.make_async_remote_copy(
+            src_ref=source(),
+            dst_ref=target(),
+            send_sem=c_send.at[array, piece, kind, level],
+            recv_sem=c_recv.at[array, piece, kind, level],
+            device_id=place,
             device_id_type=MESH,
         )
-        copy.start()
-        copies[array, kind, level] = copy
-
-    def block(level, position):
-        return rows_of((2 - level) * PLANE + position, length)
+
+    def final_copies(array, piece):
+        target = (dk_out, dv_out)[array]
+        width = final.shape[2]
+        source = final.at[array, slab(piece), :]
+        cols = rows_of(head, width)
+        if piece == len(peers):
+            return pltpu.make_async_copy(source, target.at[:, cols], local_sems.at[1 + array])
+        return pltpu.make_async_remote_copy(
+            src_ref=source,
+            dst_ref=target.at[:, cols],
+            send_sem=x_send.at[1 + array, piece],
+            recv_sem=x_recv.at[1 + array, piece],
+            device_id={"head": peers[piece]},
+            device_id_type=MESH,
+        )
 
     for level in (2, 1, 0):
-        for array in range(2):
-            part = parts[array]
-            push(array, 0, level, part.at[block(level, diagonal), :], near_buf.at[array, level, 0], base + near)
-            push(array, 1, level, part.at[block(level, near), :], near_buf.at[array, level, 1], base + near)
+        @pl.when(plane >= level)
+        def _():
+            for piece in pieces:
+                for array in range(2):
+                    copy_of(array, piece, 0, level).start()
+                    copy_of(array, piece, 1, level).start()
     exchange(0, dq_ref, dq_out)
     for level in (2, 1, 0):
+        @pl.when(plane >= level)
+        def _():
+            for piece in pieces:
+                for array in range(2):
+                    here = slab(piece)
+                    part = parts[array]
+                    copy_of(array, piece, 0, level).wait_recv()
+                    far_sum[array, level, here] = (
+                        part[rows(level, far, piece), :].astype(jnp.float32)
+                        + near_buf[array, level, 0, here].astype(jnp.float32)
+                    ).astype(jnp.bfloat16)
+                    copy_of(array, piece, 2, level).start()
+    for level in (2, 1, 0):
+        for piece in pieces:
+            for array in range(2):
+                here = slab(piece)
+                part = parts[array]
+
+                @pl.when(plane >= level)
+                def _():
+                    copy_of(array, piece, 1, level).wait_recv()
+                    copy_of(array, piece, 2, level).wait_recv()
+                    own_sum[array, level, here] = (
+                        part[rows(level, slot, piece), :].astype(jnp.float32)
+                        + near_buf[array, level, 1, here].astype(jnp.float32)
+                        + far_buf[array, level, here].astype(jnp.float32)
+                    )
+
+                if level < 2:
+                    @pl.when((plane >= level) & (plane < last))
+                    def _():
+                        copy_of(array, piece, 3, level + 1).wait_recv()
+                        own_sum[array, level, here] += down_buf[array, level, here].astype(jnp.float32)
+
+                if level > 0:
+                    @pl.when(plane >= level)
+                    def _():
+                        down_src[array, level - 1, here] = own_sum[array, level, here].astype(jnp.bfloat16)
+                        copy_of(array, piece, 3, level).start()
+                else:
+                    final[array, here] = own_sum[array, level, here].astype(jnp.bfloat16)
+                    final_copies(array, piece).start()
+    for level in range(3):
+        @pl.when(plane >= level)
+        def _():
+            for piece in pieces:
+                for array in range(2):
+                    for kind in (0, 1, 2) + ((3,) if level else ()):
+                        copy_of(array, piece, kind, level).wait_send()
+    for piece in pieces:
         for array in range(2):
-            part = parts[array]
-            copies[array, 0, level].wait_recv()
-            far_sum[array, level] = (
-                part[block(level, far), :].astype(jnp.float32) + near_buf[array, level, 0].astype(jnp.float32)
-            ).astype(jnp.bfloat16)
-            push(array, 2, level, far_sum.at[array, level], far_buf.at[array, level], base + far)
-    for level in (2, 1, 0):
-        for array in range(2):
-            part = parts[array]
-            copies[array, 1, level].wait_recv()
-            own_sum[array, level] = part[block(level, slot), :].astype(jnp.float32) + near_buf[
-                array, level, 1
-            ].astype(jnp.float32)
-    for level in (2, 1, 0):
-        for array in range(2):
-            copies[array, 2, level].wait_recv()
-            total = own_sum[array, level] + far_buf[array, level].astype(jnp.float32)
-            if level < 2:
-                copies[array, 3, level + 1].wait_recv()
-                total = total + down_buf[array, level].astype(jnp.float32)
-            if level > 0:
-                down_src[array, level - 1] = total.astype(jnp.bfloat16)
-                push(array, 3, level, down_src.at[array, level - 1], down_buf.at[array, level - 1], down)
-            else:
-                final[array] = total.astype(jnp.bfloat16)
-                exchange(1 + array, final.at[array], (dk_out, dv_out)[array])
+            final_copies(array, piece).wait()
     for local, remote in waits:
         local.wait()
         for copy in remote:
             copy.wait()
-    for copy in copies.values():
-        copy.wait_send()
+
+
+def settle_kernel(dq_ref, dk_ref, dv_ref, dq_out, dk_out, dv_out, sems):
+    copies = [
+        pltpu.make_async_copy(source, target, sems.at[index])
+        for index, (source, target) in enumerate(((dq_ref, dq_out), (dk_ref, dk_out), (dv_ref, dv_out)))
+    ]
+    for copy in copies:
+        copy.start()
+    for copy in copies:
+        copy.wait()
+
+
+def settle(*arrays):
+    return pl.pallas_call(
+        settle_kernel,
+        out_shape=tuple(jax.ShapeDtypeStruct(array.shape, array.dtype) for array in arrays),
+        in_specs=[pl.BlockSpec(memory_space=pltpu.VMEM)] * 3,
+        out_specs=(pl.BlockSpec(memory_space=pl.ANY),) * 3,
+        scratch_shapes=[pltpu.SemaphoreType.DMA((3,))],
+    )(*arrays)
 
 
 def reduce(grad_query, part_keys, part_values):
@@ -353,7 +473,7 @@
             pltpu.VMEM((2, 2) + block, jnp.bfloat16),
             pltpu.VMEM((2, 2) + block, jnp.bfloat16),
             pltpu.VMEM((2,) + block, jnp.bfloat16),
-            dma((3,)), dma((3, heads)), dma((3, heads)), dma((2, 4, 3)), dma((2, 4, 3)),
+            dma((3,)), dma((3, heads)), dma((3, heads)), dma((2, heads, 4, 3)), dma((2, heads, 4, 3)),
         ],
         compiler_params=pltpu.CompilerParams(
             collective_id=1, has_side_effects=True, vmem_limit_bytes=VMEM_LIMIT
@@ -363,10 +483,8 @@
 
 def on_device(queries, keys, values, output_cotangent, doc_ids):
     query_rows, grad_rows, key_window, value_window = gather(queries, output_cotangent, keys, values)
-    length = query_rows.shape[0]
-    own_docs = lax.dynamic_slice_in_dim(doc_ids, lax.axis_index("ctx") * length, length, 0)
-    bound = jnp.sum((doc_ids[:, None] < own_docs[None, :]).astype(jnp.int32), axis=0)[None]
-    return reduce(*attention(query_rows, grad_rows, key_window, value_window, bound))
+    docs = doc_ids.reshape(-1, key_window.shape[1])
+    return settle(*reduce(*attention(query_rows, grad_rows, key_window, value_window, docs)))
 
 
 def solution(mesh):

time: 82.2 us -> 74.1 us (0.901)
  local copies, waits for them, and re-layouts: 3.95 us -> 0 us
  other arithmetic: 3.03 us -> 0 us
  Pallas kernels: 74.2 us -> 73.2 us
    unnamed x7 -> x0, local copies, waits for them, and re-layouts: 3.18 us -> none
    reduce_sum x1 -> x0, other arithmetic: 3.03 us -> none  [on_device(): jnp.sum((doc_ids[:, None] < own_docs[None, :]).astype(jnp.int32), axis=0)]
    pallas_call x0 -> x1, Pallas kernels: none -> 1.93 us  [settle(): pl.pallas_call(settle_kernel, out_shape=tuple((jax.ShapeDtypeStruct(array...]
    pallas_call x1, Pallas kernels: 25.1 us -> 23.4 us  [gather(): pl.pallas_call(gather_kernel, out_shape=(rows, rows, window, window), in_...]
    pallas_call x1, Pallas kernels: 19.5 us -> 17.9 us  [reduce(): pl.pallas_call(reduce_kernel, out_shape=(jax.ShapeDtypeStruct((tokens, wi...]
where the time goes in v3:
time: 74.1 us; the launch traced here: 73.9 us
  Pallas kernels  73.2 us (99%)
    pallas_call x1, Pallas kernels, attention(): pl.pallas_call(functools.partial(attention_kernel, scaling=width ** (-0.5...  30.1 us
    pallas_call x1, Pallas kernels, gather(): pl.pallas_call(gather_kernel, out_shape=(rows, rows, window, window), in_...  23.4 us
    pallas_call x1, Pallas kernels, reduce(): pl.pallas_call(reduce_kernel, out_shape=(jax.ShapeDtypeStruct((tokens, wi...  17.9 us
    pallas_call x1, Pallas kernels, settle(): pl.pallas_call(settle_kernel, out_shape=tuple((jax.ShapeDtypeStruct(array...  1.93 us

profile of v3, /device:TPU:0, one launch (start us, length us, event | category | flops | bytes accessed | tf_op | source)
XLA Modules:
  0.0 73.9 jit_solution(10617492402644615351)
XLA Ops:
  0.6 23.4 %shard_map.76 = (bf16[256,1024]{1,0:T(8,128)(2,1)}, bf16[256,1024]{1,0:T(8,128)(2,1)}, bf16[3072,128]{1,0:T(8,128)(2,1)}, bf16[3072,128]{1,0:T(8,128)(2,1)}) custom-call(bf16[128,2048]{1,0:T(8,128)(2,1)} %query_ref.1, bf16[128,2048]{1,0:T(8,128)(2,1)} %grad_ref.1, bf16[128,256]{1,0:T(8,128)(2,1)} %key_ref.1, bf16[128,256]{1,0:T(8,128)(2,1)} %value_ref.1), custom_call_target="tpu_custom_call" | custom-call | tf_op jit(solution)/shard_map/pallas_call | solution.py:189
  24.0 30.1 %shard_map.77 = (bf16[256,1024]{1,0:T(8,128)(2,1)}, bf16[3072,128]{1,0:T(8,128)(2,1)}, bf16[3072,128]{1,0:T(8,128)(2,1)}) custom-call(bf16[256,1024]{1,0:T(8,128)(2,1)} %get-tuple-element.13.query_ref, bf16[256,1024]{1,0:T(8,128)(2,1)} %get-tuple-element.14.grad_ref, bf16[3072,128]{1,0:T(8,128)(2,1)} %get-tuple-element.15.key_ref, ...), custom_call_target="tpu_custom_call" | custom-call | tf_op jit(solution)/shard_map/pallas_call | solution.py:266
  54.1 17.9 %shard_map.78 = (bf16[128,2048]{1,0:T(8,128)(2,1)}, bf16[128,256]{1,0:T(8,128)(2,1)}, bf16[128,256]{1,0:T(8,128)(2,1)}) custom-call(bf16[256,1024]{1,0:T(8,128)(2,1)} %get-tuple-element.17.dq_ref, bf16[3072,128]{1,0:T(8,128)(2,1)} %get-tuple-element.18.dk_ref, bf16[3072,128]{1,0:T(8,128)(2,1)} %get-tuple-element.19.dv_ref), custom_call_target="tpu_custom_call" | custom-call | tf_op jit(solution)/shard_map/pallas_call | solution.py:463
  72.0 1.9 %shard_map.79 = (bf16[128,2048]{1,0:T(8,128)(2,1)}, bf16[128,256]{1,0:T(8,128)(2,1)}, bf16[128,256]{1,0:T(8,128)(2,1)}) custom-call(bf16[128,2048]{1,0:T(8,128)(2,1)} %get-tuple-element.20.dq_ref, bf16[128,256]{1,0:T(8,128)(2,1)} %get-tuple-element.21.dk_ref, bf16[128,256]{1,0:T(8,128)(2,1)} %get-tuple-element.22.dv_ref), custom_call_target="tpu_custom_call" | custom-call | tf_op jit(solution)/shard_map/pallas_call | solution.py:445

commit v4 on v3

--- a/solution.py
+++ b/solution.py
@@ -47,18 +47,20 @@
     return pl.ds(pl.multiple_of(index * length, length), length)
 
 
-def gather_kernel(
-    query_ref, grad_ref, key_ref, value_ref, query_out, grad_out, key_out, value_out, local_sems, x_send, x_recv, c_send, c_recv
+def attention_kernel(
+    query_in, grad_in, key_in, value_in, doc_ref, dq_ref, dk_ref, dv_ref,
+    query_ref, grad_ref, key_ref, value_ref, bias_ref, key_win, value_win, key_t_ref, value_t_ref, key_sum, value_sum,
+    local_sems, x_send, x_recv, q_send, q_recv, c_send, c_recv, *, scaling
 ):
     ctx, head, slot, base, up, down, near, far, diagonal = places()
     peers = head_peers(head)
-    tokens = key_ref.shape[0]
+    tokens = key_in.shape[0]
     length = tokens * lax.axis_size("head")
     pairs = [
-        (key_ref, key_out, slot + SPAN),
-        (value_ref, value_out, slot + SPAN),
-        (query_ref, query_out, 0),
-        (grad_ref, grad_out, 0),
+        (key_in, key_ref, slot + SPAN),
+        (value_in, value_ref, slot + SPAN),
+        (query_in, query_ref, 0),
+        (grad_in, grad_ref, 0),
     ]
     greet(
         [{"head": peer} for peer in peers]
@@ -69,7 +71,7 @@
         width = target.shape[1]
         start = pl.multiple_of(block * length + head * tokens, tokens)
         copies = []
-        for step, peer in enumerate(peers):
+        for step, peer in enumerate(peers if index < 2 else []):
             copy = pltpu.make_async_remote_copy(
                 src_ref=source.at[:, rows_of(peer, width)],
                 dst_ref=target.at[pl.ds(start, tokens), :],
@@ -86,6 +88,32 @@
         local.start()
         x_copies.append((local, copies))
 
+    width = key_ref.shape[1]
+    group_size = query_ref.shape[1] // width
+    rows_here = pl.ds(pl.multiple_of(head * tokens, tokens), tokens)
+
+    def head_copies(g):
+        copies = []
+        for array, (source, target) in enumerate(((query_in, query_ref), (grad_in, grad_ref))):
+            for step, peer in enumerate(peers):
+                columns = pl.ds(pl.multiple_of((peer * group_size + g) * width, width), width)
+                copies.append(
+                    pltpu.make_async_remote_copy(
+                        src_ref=source.at[:, columns],
+                        dst_ref=target.at[rows_here, pl.ds(pl.multiple_of(g * width, width), width)],
+                        send_sem=q_send.at[array, step, g],
+                        recv_sem=q_recv.at[array, step, g],
+                        device_id={"head": peer},
+                        device_id_type=MESH,
+                    )
+                )
+        return copies
+
+    @pl.loop(0, group_size)
+    def _(g):
+        for copy in head_copies(g):
+            copy.start()
+
     def arrive_local(index):
         x_copies[index][0].wait()
 
@@ -94,7 +122,7 @@
     order = [head] + [lax.rem(head + len(peers) + 1 - step, len(peers) + 1) for step in range(1, len(peers) + 1)]
 
     def copy_of(array, piece, kind, level):
-        target = (key_out, value_out)[array]
+        target = (key_ref, value_ref)[array]
         block, shift, partner = (
             (slot, 1, up), (slot, 0, base + far), (slot, 0, base + near), (far, 0, base + near)
         )[kind]
@@ -131,83 +159,8 @@
             else:
                 x_copies[array][1][piece - 1].wait_recv()
             spread(array, piece, 0)
-    for level in (1, 2):
-        for piece in pieces:
-            @pl.when(plane >= level)
-            def _():
-                for array in range(2):
-                    copy_of(array, piece, 0, level - 1).wait_recv()
-                    spread(array, piece, level)
-
-            for array in range(2):
-                if level == 1:
-                    relay(array, piece, 0)
-                else:
-                    @pl.when(plane >= 1)
-                    def _():
-                        relay(array, piece, 1)
-
-    @pl.when(plane >= 2)
-    def _():
-        for piece in pieces:
-            for array in range(2):
-                relay(array, piece, 2)
-
-    for level in range(3):
-        @pl.when(plane >= level)
-        def _():
-            for piece in pieces:
-                for array in range(2):
-                    copy_of(array, piece, 1, level).wait_send()
-                    copy_of(array, piece, 2, level).wait()
-                    copy_of(array, piece, 3, level).wait()
-            if level < 2:
-                @pl.when(plane < last)
-                def _():
-                    for piece in pieces:
-                        for array in range(2):
-                            copy_of(array, piece, 0, level).wait_send()
-
-    for index, (local, remote) in enumerate(x_copies):
-        if index >= 2:
-            local.wait()
-            for copy in remote:
-                copy.wait_recv()
-        for copy in remote:
-            copy.wait_send()
-
-
-def gather(queries, output_cotangent, keys, values):
-    heads = lax.axis_size("head")
-    tokens, width = queries.shape
-    length = tokens * heads
-    head_width = keys.shape[1] // heads
-    vmem = pl.BlockSpec(memory_space=pltpu.VMEM)
-    rows = jax.ShapeDtypeStruct((length, width // heads), jnp.bfloat16)
-    window = jax.ShapeDtypeStruct((SLOTS * length, head_width), jnp.bfloat16)
-    dma = pltpu.SemaphoreType.DMA
-    return pl.pallas_call(
-        gather_kernel,
-        out_shape=(rows, rows, window, window),
-        in_specs=[vmem] * 4,
-        out_specs=(vmem,) * 4,
-        scratch_shapes=[dma((4,)), dma((4, heads)), dma((4, heads)), dma((2, heads, 4, 3)), dma((2, heads, 4, 3))],
-        compiler_params=pltpu.CompilerParams(
-            collective_id=0, has_side_effects=True, vmem_limit_bytes=VMEM_LIMIT
-        ),
-    )(queries, output_cotangent, keys, values)
-
-
-def attention_kernel(
-    query_ref, grad_ref, key_ref, value_ref, doc_ref, dq_ref, dk_ref, dv_ref,
-    bias_ref, key_win, value_win, key_t_ref, value_t_ref, key_sum, value_sum, *, scaling
-):
-    length = query_ref.shape[0]
-    width = key_ref.shape[1]
     window = key_sum.shape[0]
-    group_size = query_ref.shape[1] // width
-    own_block = lax.axis_index("ctx")
-    slot = lax.rem(own_block, PLANE)
+    own_block = ctx
     reach = pl.ds(pl.multiple_of(slot * length, length), window)
     first_key = (own_block - SPAN) * length
     lanes = doc_ref.shape[1]
@@ -223,6 +176,38 @@
         key_pos = first_key + i * lanes + lax.broadcasted_iota(jnp.int32, (lanes, length), 0)
         allowed = (key_docs == query_docs) & (key_pos <= query_pos) & (key_pos >= 0)
         bias_ref[i * lanes : (i + 1) * lanes, :] = jnp.where(allowed, 0.0, masked_score)
+    for level in (1, 2):
+        for piece in pieces:
+            @pl.when(plane >= level)
+            def _():
+                for array in range(2):
+                    copy_of(array, piece, 0, level - 1).wait_recv()
+                    spread(array, piece, level)
+
+            for array in range(2):
+                if level == 1:
+                    relay(array, piece, 0)
+                else:
+                    @pl.when(plane >= 1)
+                    def _():
+                        relay(array, piece, 1)
+
+    @pl.when(plane >= 2)
+    def _():
+        for piece in pieces:
+            for array in range(2):
+                relay(array, piece, 2)
+
+    for level in range(3):
+        @pl.when(plane >= level)
+        def _():
+            for piece in pieces:
+                for array in range(2):
+                    copy_of(array, piece, 2, level).wait_recv()
+                    copy_of(array, piece, 3, level).wait_recv()
+
+    for index in (2, 3):
+        arrive_local(index)
     present = first_key + lax.broadcasted_iota(jnp.int32, (window, width), 0) >= 0
     key_win[...] = jnp.where(present, key_ref[reach, :].astype(jnp.float32), 0.0).astype(jnp.bfloat16)
     value_win[...] = jnp.where(present, value_ref[reach, :].astype(jnp.float32), 0.0).astype(jnp.bfloat16)
@@ -234,6 +219,8 @@
 
     @pl.loop(0, group_size)
     def _(g):
+        for copy in head_copies(g):
+            copy.wait_recv()
         cols = pl.ds(pl.multiple_of(g * width, width), width)
         query = query_ref[:, cols]
         grad = grad_ref[:, cols]
@@ -256,19 +243,52 @@
     dk_ref[reach, :] = (key_sum[...] * scaling).astype(jnp.bfloat16)
     dv_ref[reach, :] = value_sum[...].astype(jnp.bfloat16)
 
-
-def attention(query_rows, grad_rows, key_window, value_window, docs):
-    length = query_rows.shape[0]
-    width = key_window.shape[1]
+    for level in range(3):
+        @pl.when(plane >= level)
+        def _():
+            for piece in pieces:
+                for array in range(2):
+                    copy_of(array, piece, 1, level).wait_send()
+                    copy_of(array, piece, 2, level).wait_send()
+                    copy_of(array, piece, 3, level).wait_send()
+            if level < 2:
+                @pl.when(plane < last)
+                def _():
+                    for piece in pieces:
+                        for array in range(2):
+                            copy_of(array, piece, 0, level).wait_send()
+
+    for _, remote in x_copies:
+        for copy in remote:
+            copy.wait_send()
+
+    @pl.loop(0, group_size)
+    def _(g):
+        for copy in head_copies(g):
+            copy.wait_send()
+
+
+def attention(queries, output_cotangent, keys, values, docs):
+    heads = lax.axis_size("head")
+    tokens, query_width = queries.shape
+    length = tokens * heads
+    width = keys.shape[1] // heads
+    group_size = query_width // heads // width
     window = (SPAN + 1) * length
     vmem = pl.BlockSpec(memory_space=pltpu.VMEM)
-    parts = jax.ShapeDtypeStruct(key_window.shape, jnp.bfloat16)
+    dma = pltpu.SemaphoreType.DMA
+    rows = (length, query_width // heads)
+    parts = jax.ShapeDtypeStruct((SLOTS * length, width), jnp.bfloat16)
     return pl.pallas_call(
         functools.partial(attention_kernel, scaling=width ** (-0.5)),
-        out_shape=(jax.ShapeDtypeStruct(query_rows.shape, jnp.bfloat16), parts, parts),
+        out_shape=(jax.ShapeDtypeStruct(rows, jnp.bfloat16), parts, parts),
         in_specs=[vmem] * 5,
         out_specs=(vmem,) * 3,
         scratch_shapes=[
+            pltpu.VMEM(rows, jnp.bfloat16),
+            pltpu.VMEM(rows, jnp.bfloat16),
+            pltpu.VMEM((SLOTS * length, width), jnp.bfloat16),
+            pltpu.VMEM((SLOTS * length, width), jnp.bfloat16),
             pltpu.VMEM((window, length), jnp.float32),
             pltpu.VMEM((window, width), jnp.bfloat16),
             pltpu.VMEM((window, width), jnp.bfloat16),
@@ -276,9 +296,14 @@
             pltpu.VMEM((width, window), jnp.bfloat16),
             pltpu.VMEM((window, width), jnp.float32),
             pltpu.VMEM((window, width), jnp.float32),
+            dma((4,)), dma((2, heads)), dma((2, heads)),
+            dma((2, heads, group_size)), dma((2, heads, group_size)),
+            dma((2, heads, 4, 3)), dma((2, heads, 4, 3)),
         ],
-        compiler_params=pltpu.CompilerParams(vmem_limit_bytes=VMEM_LIMIT),
-    )(query_rows, grad_rows, key_window, value_window, docs)
+        compiler_params=pltpu.CompilerParams(
+            collective_id=0, has_side_effects=True, vmem_limit_bytes=VMEM_LIMIT
+        ),
+    )(queries, output_cotangent, keys, values, docs)
 
 
 def reduce_kernel(
@@ -482,9 +507,8 @@
 
 
 def on_device(queries, keys, values, output_cotangent, doc_ids):
-    query_rows, grad_rows, key_window, value_window = gather(queries, output_cotangent, keys, values)
-    docs = doc_ids.reshape(-1, key_window.shape[1])
-    return settle(*reduce(*attention(query_rows, grad_rows, key_window, value_window, docs)))
+    docs = doc_ids.reshape(-1, keys.shape[1] // lax.axis_size("head"))
+    return settle(*reduce(*attention(queries, output_cotangent, keys, values, docs)))
 
 
 def solution(mesh):

time: 74.1 us -> 71.1 us (0.960)
  Pallas kernels: 73.2 us -> 70.2 us
    pallas_call x1 -> x0, Pallas kernels: 23.4 us -> none  [gather(): pl.pallas_call(gather_kernel, out_shape=(rows, rows, window, window), in_...]
    pallas_call x1, Pallas kernels: 30.1 us -> 43.9 us  [attention(): pl.pallas_call(functools.partial(attention_kernel, scaling=width ** (-0.5...]
    pallas_call x1, Pallas kernels: 17.9 us -> 24.3 us  [reduce(): pl.pallas_call(reduce_kernel, out_shape=(jax.ShapeDtypeStruct((tokens, wi...]
where the time goes in v4:
time: 71.1 us; the launch traced here: 70.8 us
  Pallas kernels  70.2 us (99%)
    pallas_call x1, Pallas kernels, attention(): pl.pallas_call(functools.partial(attention_kernel, scaling=width ** (-0.5...  43.9 us
    pallas_call x1, Pallas kernels, reduce(): pl.pallas_call(reduce_kernel, out_shape=(jax.ShapeDtypeStruct((tokens, wi...  24.3 us
    pallas_call x1, Pallas kernels, settle(): pl.pallas_call(settle_kernel, out_shape=tuple((jax.ShapeDtypeStruct(array...  1.93 us

profile of v4, /device:TPU:0, one launch (start us, length us, event | category | flops | bytes accessed | tf_op | source)
XLA Modules:
  0.0 70.8 jit_solution(15062283285622504107)
XLA Ops:
  0.6 43.9 %shard_map.76 = (bf16[256,1024]{1,0:T(8,128)(2,1)}, bf16[3072,128]{1,0:T(8,128)(2,1)}, bf16[3072,128]{1,0:T(8,128)(2,1)}) custom-call(bf16[128,2048]{1,0:T(8,128)(2,1)} %query_in.1, bf16[128,2048]{1,0:T(8,128)(2,1)} %grad_in.1, bf16[128,256]{1,0:T(8,128)(2,1)} %key_in.1, bf16[128,256]{1,0:T(8,128)(2,1)} %value_in.1, s32[32,128]{1,0:T(8,128)} %bitcast.1), custom_call_target="tpu_custom_call" | custom-call | tf_op jit(solution)/shard_map/pallas_call | solution.py:282
  44.6 24.3 %shard_map.77 = (bf16[128,2048]{1,0:T(8,128)(2,1)}, bf16[128,256]{1,0:T(8,128)(2,1)}, bf16[128,256]{1,0:T(8,128)(2,1)}) custom-call(bf16[256,1024]{1,0:T(8,128)(2,1)} %get-tuple-element.9.dq_ref, bf16[3072,128]{1,0:T(8,128)(2,1)} %get-tuple-element.10.dk_ref, bf16[3072,128]{1,0:T(8,128)(2,1)} %get-tuple-element.11.dv_ref), custom_call_target="tpu_custom_call" | custom-call | tf_op jit(solution)/shard_map/pallas_call | solution.py:488
  68.9 1.9 %shard_map.78 = (bf16[128,2048]{1,0:T(8,128)(2,1)}, bf16[128,256]{1,0:T(8,128)(2,1)}, bf16[128,256]{1,0:T(8,128)(2,1)}) custom-call(bf16[128,2048]{1,0:T(8,128)(2,1)} %get-tuple-element.12.dq_ref, bf16[128,256]{1,0:T(8,128)(2,1)} %get-tuple-element.13.dk_ref, bf16[128,256]{1,0:T(8,128)(2,1)} %get-tuple-element.14.dv_ref), custom_call_target="tpu_custom_call" | custom-call | tf_op jit(solution)/shard_map/pallas_call | solution.py:470
